TPU v7x, 32 devices: a whole 2x2x4 slice. The times are simulated.
32 devices in a mesh: dp: 16 (over z, y, x), mp: 2 (over core).
Axes of the slice: x: 2, y: 2, z: 4, core: 2. Of those that a mesh axis runs over, the one named last changes fastest.
Arguments:
- inputs: bfloat16 [6144, 768], P('dp')
- cotangent: bfloat16 [6144, 768], P('dp'), may hold values from -6 to 6
- lengths: int32 [16, 3], P('dp'), may hold values from 0 to 192, as said below
- masked: int32 [6144], P('dp'), may hold values 0 or 1
- replace_ids: int32 [6144], P('dp'), may hold values from 0 to 15359, as said below
- attention_master: float32 [4, 768, 768], P(None, 'dp', 'mp')
- attention_moment: float32 [4, 768, 768], P(None, 'dp', 'mp'), may hold values from -0.1875 to 0.1875
- attention_square: float32 [4, 768, 768], P(None, 'dp', 'mp'), may hold values from 0.00016276042 to 0.0006510417
- geglu_master: float32 [3, 768, 3072], P(None, 'dp', 'mp')
- geglu_moment: float32 [3, 768, 3072], P(None, 'dp', 'mp'), may hold values from -0.1875 to 0.1875
- geglu_square: float32 [3, 768, 3072], P(None, 'dp', 'mp'), may hold values from 0.00016276042 to 0.0006510417
- embed_master: float32 [15360, 768], P('dp', 'mp'), may hold values from -6 to 6
- embed_moment: float32 [15360, 768], P('dp', 'mp'), may hold values from -0.0008544922 to 0.0008544922
- embed_square: float32 [15360, 768], P('dp', 'mp'), may hold values from 3.1789145e-09 to 1.2715658e-08
- norms_master: float32 [4, 768], replicated
- norms_moment: float32 [4, 768], replicated, may hold values from -0.1875 to 0.1875
- norms_square: float32 [4, 768], replicated, may hold values from 0.00016276042 to 0.0006510417
Outputs:
- output: float32 [6144, 768], P('dp')
- input_grad: float32 [6144, 768], P('dp')
- rms_stats: float32 [3], replicated
- lamb_norms: float32 [2, 12], replicated
- attention_grad: float32 [4, 768, 768], P(None, 'dp', 'mp')
- attention_first: float32 [4, 768, 768], P(None, 'dp', 'mp')
- attention_second: float32 [4, 768, 768], P(None, 'dp', 'mp')
- attention_new: float32 [4, 768, 768], P(None, 'dp', 'mp')
- geglu_grad: float32 [3, 768, 3072], P(None, 'dp', 'mp')
- geglu_first: float32 [3, 768, 3072], P(None, 'dp', 'mp')
- geglu_second: float32 [3, 768, 3072], P(None, 'dp', 'mp')
- geglu_new: float32 [3, 768, 3072], P(None, 'dp', 'mp')
- embed_grad: float32 [15360, 768], P('dp', 'mp')
- embed_first: float32 [15360, 768], P('dp', 'mp')
- embed_second: float32 [15360, 768], P('dp', 'mp')
- embed_new: float32 [15360, 768], P('dp', 'mp')
- norms_grad: float32 [4, 768], replicated
- norms_first: float32 [4, 768], replicated
- norms_second: float32 [4, 768], replicated
- norms_new: float32 [4, 768], replicated
Inputs may be any that keep to these rules, and one draw needn't show every extreme that they name: Row d lists the lengths of the sequences given to device d, zeros after; each sequence has 128 tokens or more; a row sums to at most 384, and some row reaches it with a sequence of 192. `replace_ids`: among the 384 slots of one device, exactly 24 ids fall in each aligned block of 960 table rows.
All inputs are finite; a program needn't handle non-finite values. No bound on the sum of `masked` on one device may be relied on, other than what follows from the above.
Results may differ from a plain program's by a relative error of at most 0.016.
The roundings to bfloat16 on the way count: a program that leaves them out, or rounds other values in their place, can miss the bound.
Values may be sent and summed in bfloat16 or wider, within the bound.
A program may use at most 192 MiB of HBM per device.

v0:
```python
import math

import jax
import jax.numpy as jnp
from jax import lax
from jax.sharding import PartitionSpec as P

HEADS = 12
STEP_COUNT = 6


first_decay = 0.5
second_decay = 0.5
learn_rate = 0.3
matrix_decay = 0.01
adam_epsilon = 1e-06
norm_epsilon = 1e-12
masked_score = -1000000000.0


def cut_along(value, dim, length):
    dims = value.shape
    tiles = value.reshape(*dims[:dim], length, dims[dim] // length, *dims[dim + 1 :])
    return jnp.moveaxis(tiles, dim, 0)


def sent_and_summed(value, axis, dim):
    length = lax.axis_size(axis)
    tiles = lax.all_to_all(cut_along(value, dim, length), axis, 0, 0, tiled=True)
    return jnp.sum(tiles.astype(jnp.float32), axis=0)


def layer_norm(values, gain_row, shift_row):
    center = values - jnp.mean(values, axis=-1, keepdims=True)
    spread = jnp.mean(center * center, axis=-1, keepdims=True)
    return center * lax.rsqrt(spread + norm_epsilon) * gain_row + shift_row


def norm_pair(values, gain_pair):
    return layer_norm(values, gain_pair[0], gain_pair[1])


def lamb_parts(master, moment, square, gradient, decay_rate):
    new_moment = first_decay * moment + (1.0 - first_decay) * gradient
    new_square = second_decay * square + (1.0 - second_decay) * gradient * gradient
    update = (
        new_moment
        / (1.0 - first_decay**STEP_COUNT)
        / (jnp.sqrt(new_square / (1.0 - second_decay**STEP_COUNT)) + adam_epsilon)
        + decay_rate * master
    )
    return (new_moment, new_square, update)


def gelu_tanh(values):
    return jax.nn.gelu(values, approximate=True)


def local(
    inputs,
    cotangent,
    lengths,
    masked,
    replace_ids,
    attention_master,
    attention_moment,
    attention_square,
    geglu_master,
    geglu_moment,
    geglu_square,
    embed_master,
    embed_moment,
    embed_square,
    norms_master,
    norms_moment,
    norms_square,
):
    half_type = jnp.bfloat16
    full_type = jnp.float32
    tokens_here = inputs.shape[0]
    width = inputs.shape[1]
    head_dim = width // HEADS
    local_heads = HEADS // lax.axis_size("mp")
    block_len = min(tokens_here, 512)
    attn_scale = 1.0 / math.sqrt(head_dim)
    column_count = embed_master.shape[1]
    attn_low, geglu_low = (
        lax.all_gather(attention_master.astype(half_type), "dp", axis=1, tiled=True),
        lax.all_gather(geglu_master.astype(half_type), "dp", axis=1, tiled=True),
    )
    table_low = lax.all_gather(embed_master.astype(half_type), "dp", axis=0, tiled=True)
    looked_cols = jnp.take(table_low, replace_ids, axis=0)
    looked = lax.all_gather(looked_cols, "mp", axis=1, tiled=True)
    is_masked = masked[:, None] == 1
    hidden_in = jnp.where(is_masked, looked.astype(full_type), inputs.astype(full_type))
    length_row = lengths[0]
    places = jnp.arange(tokens_here, dtype=jnp.int32)
    ends_at = jnp.cumsum(length_row)
    segment_ids = jnp.sum((ends_at[None, :] <= places[:, None]).astype(jnp.int32), axis=1)
    live_rows = (places < jnp.sum(length_row)).astype(full_type)[:, None]
    token_count = jnp.sum(length_row).astype(full_type)
    head_ids = lax.axis_index("mp") * local_heads + jnp.arange(local_heads, dtype=jnp.int32)
    slopes = 2.0 ** (-8.0 * (head_ids.astype(full_type) + 1.0) / HEADS)
    act_low = hidden_in.astype(half_type)
    qkv_low = jnp.einsum(
        "td,kdc->ktc", act_low, attn_low[:3], preferred_element_type=full_type
    ).astype(half_type)
    head_vals = qkv_low.reshape(3, tokens_here, local_heads, head_dim)

    def block_scores(begin_at, query_blk):
        query_pos = begin_at + jnp.arange(block_len, dtype=jnp.int32)
        scores = (
            jnp.einsum("qhe,khe->hqk", query_blk, head_vals[1], preferred_element_type=full_type)
            * attn_scale
        )
        distance = jnp.abs(query_pos[:, None] - places[None, :]).astype(full_type)
        scores = scores - slopes[:, None, None] * distance[None]
        same_seq = segment_ids[:, None] == segment_ids[None, :]
        return jnp.where(same_seq[None], scores, masked_score)

    def forward_block(begin_at):
        query_blk = head_vals[0]
        scores = block_scores(begin_at, query_blk)
        top_score = jnp.max(scores, axis=-1, keepdims=True)
        raised = jnp.exp(scores - top_score)
        row_total = jnp.sum(raised, axis=-1, keepdims=True)
        weights = (raised / row_total).astype(half_type)
        context_blk = jnp.einsum(
            "hqk,khe->qhe", weights, head_vals[2], preferred_element_type=full_type
        )
        return (context_blk.astype(half_type), (top_score + jnp.log(row_total))[..., 0])

    starts = jnp.arange(tokens_here // block_len, dtype=jnp.int32) * block_len
    context_blocks, lse_blocks = lax.map(forward_block, starts)
    context = context_blocks.reshape(tokens_here, local_heads * head_dim)
    attn_part = jnp.einsum("tc,dc->td", context, attn_low[3], preferred_element_type=full_type)
    attn_out = lax.psum(attn_part, "mp")
    normed_one, first_back = jax.vjp(norm_pair, hidden_in + attn_out, norms_master[0:2])
    normed_low = normed_one.astype(half_type)
    gate_up = jnp.einsum("td,kdf->ktf", normed_low, geglu_low[:2], preferred_element_type=full_type)
    gelu_val, gelu_back = jax.vjp(gelu_tanh, gate_up[0])
    inner_act = (gelu_val * gate_up[1]).astype(half_type)
    geglu_part = jnp.einsum("tf,df->td", inner_act, geglu_low[2], preferred_element_type=full_type)
    geglu_out = lax.psum(geglu_part, "mp")
    result, second_back = jax.vjp(norm_pair, normed_one + geglu_out, norms_master[2:4])
    squares = jnp.stack(
        [
            jnp.sum(hidden_in * hidden_in * live_rows),
            jnp.sum(attn_out * attn_out * live_rows),
            jnp.sum(geglu_out * geglu_out * live_rows),
        ]
    )
    count_total, square_total = lax.psum((token_count, squares), "dp")
    rms_stats = jnp.sqrt(square_total / (count_total * width) + 1e-06)
    grad_second, norm_grad_two = second_back(cotangent.astype(full_type) * live_rows)
    grad_geglu = grad_second.astype(half_type)
    grad_inner = jnp.einsum("td,df->tf", grad_geglu, geglu_low[2], preferred_element_type=full_type)
    down_grad = jnp.einsum("td,tf->df", grad_geglu, inner_act, preferred_element_type=full_type)
    grad_gate = gelu_back(grad_inner * gate_up[1])[0]
    grad_up = grad_inner * gelu_val
    grad_gu = jnp.stack([grad_gate, grad_up]).astype(half_type)
    gu_grad = jnp.einsum("td,ktf->kdf", normed_low, grad_gu, preferred_element_type=full_type)
    geglu_local = jnp.concatenate([gu_grad, down_grad[None]], axis=0)
    back_part = jnp.einsum("ktf,kdf->td", grad_gu, geglu_low[:2], preferred_element_type=full_type)
    grad_normed = grad_second + lax.psum(back_part, "mp")
    grad_first_in, norm_grad_one = first_back(grad_normed)
    grad_attn = grad_first_in.astype(half_type)
    grad_context = jnp.einsum(
        "td,dc->tc", grad_attn, attn_low[3], preferred_element_type=full_type
    ).astype(half_type)
    out_grad = jnp.einsum("td,tc->dc", grad_attn, context, preferred_element_type=full_type)
    grad_heads = grad_context.reshape(tokens_here, local_heads, head_dim)

    def backward_block(carry, packed):
        key_acc, value_acc = carry
        begin_at, lse_blk = packed
        query_blk = head_vals[0]
        scores = block_scores(begin_at, query_blk)
        weights = jnp.exp(scores - lse_blk[..., None])
        grad_weights = jnp.einsum(
            "qhe,khe->hqk", grad_heads, head_vals[2], preferred_element_type=full_type
        )
        value_acc = value_acc + jnp.einsum(
            "hqk,qhe->khe", weights.astype(half_type), grad_heads, preferred_element_type=full_type
        )
        row_inner = jnp.sum(grad_weights * weights, axis=-1, keepdims=True)
        grad_scores = (weights * (grad_weights - row_inner)).astype(half_type)
        grad_query = (
            jnp.einsum("hqk,khe->qhe", grad_scores, head_vals[1], preferred_element_type=full_type)
            * attn_scale
        )
        key_acc = (
            key_acc
            + jnp.einsum("hqk,qhe->khe", grad_scores, query_blk, preferred_element_type=full_type)
            * attn_scale
        )
        return ((key_acc, value_acc), grad_query.astype(half_type))

    zero_heads = jnp.zeros((tokens_here, local_heads, head_dim), full_type)
    (key_acc, value_acc), query_grads = lax.scan(
        backward_block, (zero_heads, zero_heads), (starts, lse_blocks)
    )
    grad_qkv = jnp.stack(
        [
            query_grads.reshape(tokens_here, -1),
            key_acc.reshape(tokens_here, -1).astype(half_type),
            value_acc.reshape(tokens_here, -1).astype(half_type),
        ]
    )
    qkv_grad = jnp.einsum("td,ktc->kdc", act_low, grad_qkv, preferred_element_type=full_type)
    act_part = jnp.einsum("ktc,kdc->td", grad_qkv, attn_low[:3], preferred_element_type=full_type)
    grad_in = grad_first_in + lax.psum(act_part.astype(jnp.bfloat16), "mp").astype(jnp.float32)
    input_grad = jnp.where(is_masked, 0.0, grad_in)
    attention_local = jnp.concatenate([qkv_grad, out_grad[None]], axis=0)
    own_columns = lax.dynamic_slice_in_dim(
        grad_in, lax.axis_index("mp") * column_count, column_count, 1
    )
    picked = jnp.where(is_masked, own_columns, 0.0)
    embed_local = jax.ops.segment_sum(picked, replace_ids, num_segments=table_low.shape[0])
    embed_summed = lax.psum_scatter(embed_local, "dp", scatter_dimension=0, tiled=True)
    attention_summed, geglu_summed = (
        sent_and_summed(attention_local.astype(jnp.bfloat16), "dp", 1),
        sent_and_summed(geglu_local.astype(jnp.bfloat16), "dp", 1),
    )
    inverse_count = 1.0 / count_total
    attention_grad = attention_summed * inverse_count
    geglu_grad = geglu_summed * inverse_count
    embed_grad = embed_summed * inverse_count
    attention_first, attention_second, attention_update = lamb_parts(
        attention_master, attention_moment, attention_square, attention_grad, matrix_decay
    )
    geglu_first, geglu_second, geglu_update = lamb_parts(
        geglu_master, geglu_moment, geglu_square, geglu_grad, matrix_decay
    )
    embed_first, embed_second, embed_update = lamb_parts(
        embed_master, embed_moment, embed_square, embed_grad, matrix_decay
    )
    weight_squares = jnp.concatenate(
        [
            jnp.sum(attention_master * attention_master, axis=(1, 2)),
            jnp.sum(geglu_master * geglu_master, axis=(1, 2)),
            jnp.sum(embed_master * embed_master)[None],
        ]
    )
    update_squares = jnp.concatenate(
        [
            jnp.sum(attention_update * attention_update, axis=(1, 2)),
            jnp.sum(geglu_update * geglu_update, axis=(1, 2)),
            jnp.sum(embed_update * embed_update)[None],
        ]
    )
    norms_local = jnp.concatenate([norm_grad_one, norm_grad_two], axis=0)
    weight_total, update_total, norms_summed = lax.psum(
        (weight_squares, update_squares, norms_local * 0.5), ("dp", "mp")
    )
    weight_norms = jnp.sqrt(weight_total)
    update_norms = jnp.sqrt(update_total)
    ratios = weight_norms / update_norms
    attention_new = attention_master - learn_rate * ratios[0:4][:, None, None] * attention_update
    geglu_new = geglu_master - learn_rate * ratios[4:7][:, None, None] * geglu_update
    embed_new = embed_master - learn_rate * ratios[7] * embed_update
    norms_grad = norms_summed * inverse_count
    norms_first, norms_second, norms_update = lamb_parts(
        norms_master, norms_moment, norms_square, norms_grad, 0.0
    )
    norm_weight = jnp.sqrt(jnp.sum(norms_master * norms_master, axis=1))
    norm_update = jnp.sqrt(jnp.sum(norms_update * norms_update, axis=1))
    norms_new = norms_master - learn_rate * (norm_weight / norm_update)[:, None] * norms_update
    lamb_norms = jnp.stack(
        [jnp.concatenate([weight_norms, norm_weight]), jnp.concatenate([update_norms, norm_update])]
    )
    return (
        result,
        input_grad,
        rms_stats,
        lamb_norms,
        attention_grad,
        attention_first,
        attention_second,
        attention_new,
        geglu_grad,
        geglu_first,
        geglu_second,
        geglu_new,
        embed_grad,
        embed_first,
        embed_second,
        embed_new,
        norms_grad,
        norms_first,
        norms_second,
        norms_new,
    )


def solution(mesh):
    in_specs = (
        P("dp", None),
        P("dp", None),
        P("dp", None),
        P("dp"),
        P("dp"),
        P(None, "dp", "mp"),
        P(None, "dp", "mp"),
        P(None, "dp", "mp"),
        P(None, "dp", "mp"),
        P(None, "dp", "mp"),
        P(None, "dp", "mp"),
        P("dp", "mp"),
        P("dp", "mp"),
        P("dp", "mp"),
        P(),
        P(),
        P(),
    )
    out_specs = (
        P("dp", None),
        P("dp", None),
        P(),
        P(),
        P(None, "dp", "mp"),
        P(None, "dp", "mp"),
        P(None, "dp", "mp"),
        P(None, "dp", "mp"),
        P(None, "dp", "mp"),
        P(None, "dp", "mp"),
        P(None, "dp", "mp"),
        P(None, "dp", "mp"),
        P("dp", "mp"),
        P("dp", "mp"),
        P("dp", "mp"),
        P("dp", "mp"),
        P(),
        P(),
        P(),
        P(),
    )
    return jax.shard_map(local, mesh=mesh, in_specs=in_specs, out_specs=out_specs, check_vma=False)
```

profile of v0, /device:TPU:0, one launch (start us, length us, event | category | flops | bytes accessed | tf_op | source)
XLA Modules:
  0.0 1077.3 jit_solution(6731088985889812064)
XLA Ops:
  7.2 1.7 copy.142
  9.1 2.3 convert_element_type.151
  13.5 62.9 %all-gather.6.cloned.1.call-done = bf16[4,768,384]{2,0,1:T(4,128)(2,1)} async-done(((bf16[4,48,384]{2,0,1:T(4,128)(2,1)}), bf16[4,768,384]{2,0,1:T(4,128)(2,1)}) %all-gather.6.cloned.1.call-update) | async-done | bytes 2359312 | tf_op jit(solution)/shard_map/all_gather | solution.py:88
  76.4 5.5 copy.136
  81.9 2.2 slice.94
  84.1 139.1 %all-gather.4.cloned.1.call-done = bf16[15360,384]{1,0:T(8,128)(2,1)} async-done(((bf16[960,384]{1,0:T(8,128)(2,1)}), bf16[15360,384]{1,0:T(8,128)(2,1)}) %all-gather.4.cloned.1.call-update) | async-done | bytes 11796496 | tf_op jit(solution)/shard_map/all_gather | solution.py:91
  223.2 7.9 gather_fusion
  231.2 2.2 all_gather.13
  239.4 1.5 fusion.69
  241.0 2.0 convert_element_type.165
  243.8 15.2 %all-reduce.11.cloned.1.call-done = f32[384,768]{1,0:T(8,128)} async-done(((f32[384,768]{1,0:T(8,128)}), f32[384,768]{1,0:T(8,128)}) %all-reduce.11.cloned.1.call-update) | async-done | bytes 1179664 | tf_op jit(solution)/shard_map/psum | solution.py:137
  259.1 2.0 fusion.92
  262.4 102.8 %all-gather.8.cloned.1.call-done = bf16[3,768,1536]{2,1,0:T(8,128)(2,1)} async-done(((bf16[3,48,1536]{2,1,0:T(8,128)(2,1)}), bf16[3,768,1536]{2,1,0:T(8,128)(2,1)}) %all-gather.8.cloned.1.call-update) | async-done | bytes 7077904 | tf_op jit(solution)/shard_map/all_gather | solution.py:89
  365.1 4.8 fusion.6
  373.1 3.8 fusion.33
  378.9 16.2 %all-reduce.13.cloned.1.call-done = f32[384,768]{1,0:T(8,128)} async-done(((f32[384,768]{1,0:T(8,128)}), f32[384,768]{1,0:T(8,128)}) %all-reduce.13.cloned.1.call-update) | async-done | bytes 1179664 | tf_op jit(solution)/shard_map/psum | solution.py:144
  395.1 2.2 fusion.90
  398.6 1.9 multiply_reduce_fusion.3
  400.5 1.7 fusion.89
  402.2 4.5 fusion.56
  408.3 3.0 fusion.39
  412.3 20.1 %all-reduce.15.cloned.1.call-done = f32[384,768]{1,0:T(8,128)} async-done(((f32[384,768]{1,0:T(8,128)}), f32[384,768]{1,0:T(8,128)}) %all-reduce.15.cloned.1.call-update) | async-done | bytes 1179664 | tf_op jit(solution)/shard_map/psum | solution.py:165
  432.5 4.1 multiply_reduce_fusion.4
  445.3 2.8 fusion.43
  448.2 20.1 %all-reduce.17.cloned.1.call-done = bf16[384,768]{1,0:T(8,128)(2,1)} async-done(((bf16[384,768]{1,0:T(8,128)(2,1)}), bf16[384,768]{1,0:T(8,128)(2,1)}) %all-reduce.17.cloned.1.call-update) | async-done | bytes 589840 | tf_op jit(solution)/shard_map/psum | solution.py:212
  468.4 2.4 broadcast_select_fusion
  470.7 12.7 %scatter_custom_fusion = f32[15360,384]{1,0:T(8,128)} fusion(s32[384]{0:T(512)} %param.21, f32[]{:T(128)} %constant.67.clone.1, f32[384,768]{1,0:T(8,128)S(1)} %get-tuple-element.110, s32[]{:T(128)} %constant.48.clone.1, s32[]{:T(128)S(6)} %select_n.36, pred[384]{0:T(512)(128)(4,1)S(1)} %copy-done.69), kind=kCustom, calls=%fused_computation.3 | custom fusion | flops 294912 | bytes 24184836 | tf_op jit(solution)/shard_map/scatter-add | solution.py:219
  484.8 2.5 convert_bitcast_fusion
  487.3 2.8 copy.118
  491.2 1.8 copy.121
  493.1 6.9 all-to-all-start
  500.0 6.5 convolution_convert_fusion
  507.9 2.6 fusion.10
  510.6 5.8 maximum_bitcast_fusion
  516.4 66.4 %all-to-all-done = bf16[16,4,48,384]{3,2,1,0:T(8,128)(2,1)S(1)} async-done(((bf16[16,4,48,384]{3,2,1,0:T(8,128)(2,1)}), bf16[16,4,48,384]{3,2,1,0:T(8,128)(2,1)S(1)}, u32[]{:S(2)}, u32[]{:S(2)}) %all-to-all-start) | async-done | bytes 2359328 | tf_op jit(solution)/shard_map/all_to_all | solution.py:29
  582.8 29.9 %all-to-all-start.1 = ((bf16[16,3,48,1536]{3,2,1,0:T(8,128)(2,1)}), bf16[16,3,48,1536]{3,2,1,0:T(8,128)(2,1)}, u32[]{:S(2)}, u32[]{:S(2)}) async-start(bf16[16,3,48,1536]{3,2,1,0:T(8,128)(2,1)} %maximum_bitcast_fusion), calls=%async_computation.1 | async-start | bytes 14155776 | tf_op jit(solution)/shard_map/all_to_all | solution.py:29
  613.5 1.9 pad_maximum_fusion.9
  615.4 219.6 %all-reduce.5 = (f32[3]{0:T(128)S(1)}, f32[]{:T(128)}) all-reduce(f32[3]{0:T(128)S(1)} %pad_maximum_fusion.9, f32[]{:T(128)S(6)} %convert_element_type.185), channel_id=1, replica_groups=mesh['dp'=16,'mp'=2] {'dp'}, use_global_device_ids=true, to_apply=%region_21.22 | all-reduce | flops 4 | bytes 32 | tf_op jit(solution)/shard_map/psum | solution.py:153
  837.9 1.7 multiply_reduce_fusion.15
  839.6 4.8 convert_reduce_fusion
  844.4 2.4 multiply_reduce_fusion.13
  846.9 165.3 %reduce-scatter.2.cloned.1.call-done = f32[960,384]{1,0:T(8,128)} async-done(((f32[15360,384]{1,0:T(8,128)}), f32[960,384]{1,0:T(8,128)}) %reduce-scatter.2.cloned.1.call-update) | async-done | bytes 1474576 | tf_op jit(solution)/shard_map/reduce_scatter | solution.py:220
  1012.2 5.4 multiply_reduce_fusion.2
  1017.7 1.9 pad_maximum_fusion.10
  1019.5 39.7 %all-reduce.4 = (f32[4,768]{1,0:T(4,128)}, f32[8]{0:T(128)}, f32[8]{0:T(128)}) all-reduce(f32[4,768]{1,0:T(4,128)} %maximum_multiply_fusion, f32[8]{0:T(128)} %get-tuple-element.142, f32[8]{0:T(128)S(1)} %get-tuple-element.141), channel_id=1, replica_groups=mesh['dp'=16,'mp'=2] {'dp','mp'}, use_global_device_ids=true, to_apply=%region_40.41 | all-reduce | flops 3088 | bytes 24704 | tf_op jit(solution)/shard_map/psum | solution.py:253
  1061.4 1.5 multiply_reduce_fusion.16
  1064.3 1.9 multiply_subtract_fusion.2
  1068.4 1.9 multiply_subtract_fusion
  (251 shorter events, 38.2 us)
Async XLA Ops:
  7.2 69.2 %all-gather.6.cloned.1.call-start = ((), (), s32[]{:S(2)}) async-start(), calls=%async_computation.4 | async-start | bytes 2506752 | tf_op jit(solution)/shard_map/all_gather | solution.py:88
  9.0 214.2 %all-gather.4.cloned.1.call-start = ((), (), s32[]{:S(2)}) async-start(), calls=%async_computation.3 | async-start | bytes 12533760 | tf_op jit(solution)/shard_map/all_gather | solution.py:91
  11.4 247.6 %all-reduce.11.cloned.1.call-start = ((), (), s32[]{:S(2)}) async-start(), calls=%async_computation.5 | async-start | bytes 2359296 | tf_op jit(solution)/shard_map/psum | solution.py:137
  12.7 220.8 %copy-start.67 = (pred[384]{0:T(512)(128)(4,1)}, pred[384]{0:T(512)(128)(4,1)S(1)}, u32[]{:S(2)}) copy-start(pred[384]{0:T(512)(128)(4,1)S(1)} %broadcast_compare_fusion.1) | copy-start | bytes 1156
  76.4 5.5 copy-start.12
  84.1 149.4 %copy-start.23 = (bf16[384,768]{1,0:T(8,128)(2,1)S(1)}, bf16[384,768]{1,0:T(8,128)(2,1)}, u32[]{:S(2)}) copy-start(bf16[384,768]{1,0:T(8,128)(2,1)} %param.17) | copy-start | bytes 1769476
  84.1 149.4 %copy-start.26 = (bf16[3,768,384]{1,2,0:T(8,128)(2,1)S(1)}, bf16[3,768,384]{1,2,0:T(8,128)(2,1)}, u32[]{:S(2)}) copy-start(bf16[3,768,384]{1,2,0:T(8,128)(2,1)} %copy.136) | copy-start | bytes 5308420
  240.9 124.2 %all-gather.8.cloned.1.call-start = ((), (), s32[]{:S(2)}) async-start(), calls=%async_computation.6 | async-start | bytes 7520256 | tf_op jit(solution)/shard_map/all_gather | solution.py:89
  243.0 152.1 %all-reduce.13.cloned.1.call-start = ((), (), s32[]{:S(2)}) async-start(), calls=%async_computation.7 | async-start | bytes 2359296 | tf_op jit(solution)/shard_map/psum | solution.py:144
  261.1 134.0 %copy-start.47 = (f32[384]{0:T(512)}, f32[384]{0:T(512)S(1)}, u32[]{:S(2)}) copy-start(f32[384]{0:T(512)S(1)} %broadcast_multiply_fusion.5) | copy-start | bytes 4612
  262.3 107.6 %copy-start.59 = (f32[384]{0:T(512)}, f32[384]{0:T(512)S(1)}, u32[]{:S(2)}) copy-start(f32[384]{0:T(512)S(1)} %multiply_reduce_fusion.11) | copy-start | bytes 4612
  262.3 132.7 %copy-start.53 = (f32[384]{0:T(512)}, f32[384]{0:T(512)S(1)}, u32[]{:S(2)}) copy-start(f32[384]{0:T(512)S(1)} %fusion.74) | copy-start | bytes 4612
  377.0 55.5 %all-reduce.15.cloned.1.call-start = ((), (), s32[]{:S(2)}) async-start(), calls=%async_computation.8 | async-start | bytes 2359296 | tf_op jit(solution)/shard_map/psum | solution.py:165
  378.9 18.7 %copy-start.52 = (f32[768]{0:T(1024)S(1)}, f32[768]{0:T(1024)}, u32[]{:S(2)}) copy-start(f32[768]{0:T(1024)} %get-tuple-element.83) | copy-start | bytes 9220
  397.3 4.9 slice-start
  400.5 7.7 slice-start.2
  402.2 4.5 copy-start.17
  402.2 4.6 copy-start.70
  402.2 6.1 slice-start.3
  411.4 57.0 %all-reduce.17.cloned.1.call-start = ((), (), s32[]{:S(2)}) async-start(), calls=%async_computation.9 | async-start | bytes 1179648 | tf_op jit(solution)/shard_map/psum | solution.py:212
  445.3 23.0 %copy-start.5 = (f32[384,768]{1,0:T(8,128)S(1)}, f32[384,768]{1,0:T(8,128)}, u32[]{:S(2)}) copy-start(f32[384,768]{1,0:T(8,128)} %copy-done.4) | copy-start | bytes 3538948
  445.3 23.0 %copy-start.58 = (f32[384]{0:T(512)S(1)}, f32[384]{0:T(512)}, u32[]{:S(2)}) copy-start(f32[384]{0:T(512)} %copy-done.57) | copy-start | bytes 4612
  445.3 23.0 %copy-start.69 = (pred[384]{0:T(512)(128)(4,1)S(1)}, pred[384]{0:T(512)(128)(4,1)}, u32[]{:S(2)}) copy-start(pred[384]{0:T(512)(128)(4,1)} %copy-done.67) | copy-start | bytes 1156
  448.2 564.0 %reduce-scatter.2.cloned.1.call-start = ((), (), s32[]{:S(2)}) async-start(), calls=%async_computation.10 | async-start | bytes 25067520 | tf_op jit(solution)/shard_map/reduce_scatter | solution.py:220
  493.0 6.9 copy-start.2
  493.0 7.0 copy-start.49
  493.1 7.0 copy-start.55
  493.1 7.0 copy-start.64
  493.1 89.8 %all-to-all-start = ((bf16[16,4,48,384]{3,2,1,0:T(8,128)(2,1)}), bf16[16,4,48,384]{3,2,1,0:T(8,128)(2,1)S(1)}, u32[]{:S(2)}, u32[]{:S(2)}) async-start(bf16[16,4,48,384]{3,2,1,0:T(8,128)(2,1)} %copy.121), calls=%async_computation | async-start | bytes 4718592 | tf_op jit(solution)/shard_map/all_to_all | solution.py:29
  516.4 318.7 %copy-start.66 = (f32[768]{0:T(1024)S(1)}, f32[768]{0:T(1024)}, u32[]{:S(2)}) copy-start(f32[768]{0:T(1024)} %get-tuple-element.73) | copy-start | bytes 9220
  516.4 320.0 %copy-start.65 = (f32[768]{0:T(1024)S(1)}, f32[768]{0:T(1024)}, u32[]{:S(2)}) copy-start(f32[768]{0:T(1024)} %get-tuple-element.80) | copy-start | bytes 9220
  516.4 320.5 %copy-start.63 = (f32[768]{0:T(1024)S(1)}, f32[768]{0:T(1024)}, u32[]{:S(2)}) copy-start(f32[768]{0:T(1024)} %get-tuple-element.71) | copy-start | bytes 9220
  516.4 320.5 %copy-start.62 = (f32[768]{0:T(1024)S(1)}, f32[768]{0:T(1024)}, u32[]{:S(2)}) copy-start(f32[768]{0:T(1024)} %get-tuple-element.77) | copy-start | bytes 9220
  582.8 256.8 %all-to-all-start.1 = ((bf16[16,3,48,1536]{3,2,1,0:T(8,128)(2,1)}), bf16[16,3,48,1536]{3,2,1,0:T(8,128)(2,1)}, u32[]{:S(2)}, u32[]{:S(2)}) async-start(bf16[16,3,48,1536]{3,2,1,0:T(8,128)(2,1)} %maximum_bitcast_fusion), calls=%async_computation.1 | async-start | bytes 14155776 | tf_op jit(solution)/shard_map/all_to_all | solution.py:29
  612.8 225.2 %copy-start.21 = (f32[4,48,384]{2,1,0:T(8,128)S(1)}, f32[4,48,384]{2,1,0:T(8,128)}, u32[]{:S(2)}) copy-start(f32[4,48,384]{2,1,0:T(8,128)} %param.22) | copy-start | bytes 884740
  612.8 225.2 %copy-start.42 = (f32[4,48,384]{2,1,0:T(8,128)S(1)}, f32[4,48,384]{2,1,0:T(8,128)}, u32[]{:S(2)}) copy-start(f32[4,48,384]{2,1,0:T(8,128)} %param.23) | copy-start | bytes 884740
  612.8 225.1 %copy-start.43 = (f32[4,48,384]{2,1,0:T(8,128)S(1)}, f32[4,48,384]{2,1,0:T(8,128)}, u32[]{:S(2)}) copy-start(f32[4,48,384]{2,1,0:T(8,128)} %param.24) | copy-start | bytes 884740
  839.6 4.8 copy-start.6
  839.6 4.8 copy-start.38
  839.6 4.8 copy-start.39
  844.4 167.8 %copy-start.3 = (f32[960,384]{1,0:T(8,128)S(1)}, f32[960,384]{1,0:T(8,128)}, u32[]{:S(2)}) copy-start(f32[960,384]{1,0:T(8,128)} %param.28) | copy-start | bytes 4423684
  846.9 219.4 %copy-start.19 = (f32[3,48,1536]{2,1,0:T(8,128)}, f32[3,48,1536]{2,1,0:T(8,128)S(1)}, u32[]{:S(2)}) copy-start(f32[3,48,1536]{2,1,0:T(8,128)S(1)} %get-tuple-element.103) | copy-start | bytes 2654212
  846.9 214.5 %copy-start.46 = (f32[4,768]{1,0:T(4,128)S(1)}, f32[4,768]{1,0:T(4,128)}, u32[]{:S(2)}) copy-start(f32[4,768]{1,0:T(4,128)} %param.31) | copy-start | bytes 36868
  1012.2 5.4 copy-start.73
  1012.2 5.4 copy-start.74
  1012.2 5.4 copy-start.75
  1012.2 5.4 copy-start.76
  1059.3 7.0 copy-start.20
  (47 other events, 94.8 us)
Sparse Core Ops, SparseCore 0:
  11.4 64.9 all-gather.5
  79.8 143.3 all-gather.3
  241.0 17.9 all-reduce.10
  262.6 102.5 all-gather.7
  377.1 17.9 all-reduce.12
  411.5 20.9 all-reduce.14
  448.3 20.0 all-reduce.16
  483.7 528.5 reduce-scatter.1
where the time goes:
time: 1080 us
  waiting for transfers between devices  608 us (56%)
  blocking collectives  262 us (24%)
  other arithmetic  73.8 us (7%)
  matrix products  39.9 us (4%)
  local copies, waits for them, and re-layouts  38.1 us (4%)
  starting transfers between devices  37.6 us (3%)
  between operations  18.1 us (2%)
    psum x1, blocking collectives, local(): count_total, square_total = lax.psum((token_count, squares), 'dp')  220 us
    reduce_scatter x1, waiting for transfers between devices, local(): lax.psum_scatter(embed_local, 'dp', scatter_dimension=0, tiled=True)  165 us
    all_gather x1, waiting for transfers between devices, local(): lax.all_gather(embed_master.astype(half_type), 'dp', axis=0, tiled=True)  139 us
    all_gather x1, waiting for transfers between devices, local(): lax.all_gather(geglu_master.astype(half_type), 'dp', axis=1, tiled=True)  103 us
    all_to_all x2, waiting for transfers between devices, sent_and_summed(): lax.all_to_all(cut_along(value, dim, length), axis, 0, 0, tiled=True)  66.4 us
    all_gather x1, waiting for transfers between devices, local(): lax.all_gather(attention_master.astype(half_type), 'dp', axis=1, tiled=True)  62.9 us
    psum x1, blocking collectives, local(): lax.psum((weight_squares, update_squares, norms_local * 0.5), ('dp', 'mp'))  39.7 us
    all_to_all x2, starting transfers between devices, sent_and_summed(): lax.all_to_all(cut_along(value, dim, length), axis, 0, 0, tiled=True)  36.9 us
  transfers between devices with their start and end apart: 10, of which 9 were waited for; matrix products, arithmetic and copies ran while one was open for 5% of the time, Pallas kernels for 0%

commit v1 on v0

--- a/solution.py
+++ b/solution.py
@@ -88,8 +88,28 @@
         lax.all_gather(attention_master.astype(half_type), "dp", axis=1, tiled=True),
         lax.all_gather(geglu_master.astype(half_type), "dp", axis=1, tiled=True),
     )
-    table_low = lax.all_gather(embed_master.astype(half_type), "dp", axis=0, tiled=True)
-    looked_cols = jnp.take(table_low, replace_ids, axis=0)
+    owners = lax.axis_size("dp")
+    owner_rows = embed_master.shape[0]
+    per_owner = tokens_here // owners
+    owner_low = jnp.arange(owners, dtype=jnp.int32)[:, None] * owner_rows
+    owned = (replace_ids[None, :] >= owner_low) & (replace_ids[None, :] < owner_low + owner_rows)
+    order = jnp.arange(tokens_here, dtype=jnp.int32)
+    earlier = (order[:, None] < order[None, :]).astype(half_type)
+    rank = jnp.dot(owned.astype(half_type), earlier, preferred_element_type=full_type)
+    owner_at = jnp.arange(owners, dtype=full_type)[:, None] * per_owner
+    target = jnp.sum(jnp.where(owned, rank + owner_at, 0.0), axis=0).astype(jnp.int32)
+    moves = target[None, :] == order[:, None]
+    sorted_ids = jnp.sum(jnp.where(moves, replace_ids[None, :], 0), axis=1)
+    asked = lax.all_to_all(sorted_ids, "dp", 0, 0, tiled=True)
+    asked = asked - lax.axis_index("dp") * owner_rows
+    hits = asked[:, None] == jnp.arange(owner_rows, dtype=jnp.int32)[None, :]
+    sent_rows = jnp.dot(
+        hits.astype(half_type), embed_master.astype(half_type), preferred_element_type=full_type
+    ).astype(half_type)
+    got_rows = lax.all_to_all(sent_rows, "dp", 0, 0, tiled=True)
+    looked_cols = jnp.einsum(
+        "pt,pc->tc", moves.astype(half_type), got_rows, preferred_element_type=full_type
+    ).astype(half_type)
     looked = lax.all_gather(looked_cols, "mp", axis=1, tiled=True)
     is_masked = masked[:, None] == 1
     hidden_in = jnp.where(is_masked, looked.astype(full_type), inputs.astype(full_type))
@@ -216,8 +236,10 @@
         grad_in, lax.axis_index("mp") * column_count, column_count, 1
     )
     picked = jnp.where(is_masked, own_columns, 0.0)
-    embed_local = jax.ops.segment_sum(picked, replace_ids, num_segments=table_low.shape[0])
-    embed_summed = lax.psum_scatter(embed_local, "dp", scatter_dimension=0, tiled=True)
+    highest = lax.Precision.HIGHEST
+    sorted_grads = jnp.dot(moves.astype(full_type), picked, precision=highest)
+    got_grads = lax.all_to_all(sorted_grads, "dp", 0, 0, tiled=True)
+    embed_summed = jnp.einsum("pr,pc->rc", hits.astype(full_type), got_grads, precision=highest)
     attention_summed, geglu_summed = (
         sent_and_summed(attention_local.astype(jnp.bfloat16), "dp", 1),
         sent_and_summed(geglu_local.astype(jnp.bfloat16), "dp", 1),

time: 1080 us -> 680 us (0.63)
  waiting for transfers between devices: 608 us -> 261 us
  blocking collectives: 262 us -> 221 us
  other arithmetic: 73.8 us -> 52.2 us
  matrix products: 39.9 us -> 52.3 us
    reduce_scatter x1 -> x0, waiting for transfers between devices: 165 us -> none  [local(): lax.psum_scatter(embed_local, 'dp', scatter_dimension=0, tiled=True)]
    all_gather x1 -> x0, waiting for transfers between devices: 139 us -> none  [local(): lax.all_gather(embed_master.astype(half_type), 'dp', axis=0, tiled=True)]
    psum x1, blocking collectives: 220 us -> 166 us  [local(): count_total, square_total = lax.psum((token_count, squares), 'dp')]
    all_to_all x2, waiting for transfers between devices: 66.4 us -> 30.5 us  [sent_and_summed(): lax.all_to_all(cut_along(value, dim, length), axis, 0, 0, tiled=True)]
    all_gather x1, waiting for transfers between devices: 62.9 us -> 32.8 us  [local(): lax.all_gather(attention_master.astype(half_type), 'dp', axis=1, tiled=True)]
    all_to_all x0 -> x3, waiting for transfers between devices: none -> 22.6 us  [the longest x1 8.82 us: local(): got_rows = lax.all_to_all(sent_rows, 'dp', 0, 0, tiled=True)]
    all_to_all x2, starting transfers between devices: 36.9 us -> 15.4 us  [sent_and_summed(): lax.all_to_all(cut_along(value, dim, length), axis, 0, 0, tiled=True)]
    all_to_all x0 -> x3, starting transfers between devices: none -> 18.7 us  [the longest x1 8.31 us: local(): asked = lax.all_to_all(sorted_ids, 'dp', 0, 0, tiled=True)]
  transfers between devices with their start and end apart: 10 -> 11, of which waited for: 9 -> 10; matrix products, arithmetic and copies ran while one was open for 5% -> 8% of each run, Pallas kernels for 0% -> 0%
where the time goes in v1:
time: 680 us; the launch traced here: 670 us
  waiting for transfers between devices  261 us (38%)
  blocking collectives  221 us (32%)
  matrix products  52.3 us (8%)
  other arithmetic  52.2 us (8%)
  starting transfers between devices  34.7 us (5%)
  local copies, waits for them, and re-layouts  30.1 us (4%)
  between operations  18.3 us (3%)
    psum x1, blocking collectives, local(): count_total, square_total = lax.psum((token_count, squares), 'dp')  166 us
    all_gather x1, waiting for transfers between devices, local(): lax.all_gather(geglu_master.astype(half_type), 'dp', axis=1, tiled=True)  103 us
    psum x1, blocking collectives, local(): lax.psum((weight_squares, update_squares, norms_local * 0.5), ('dp', 'mp'))  52.9 us
    all_gather x1, waiting for transfers between devices, local(): lax.all_gather(attention_master.astype(half_type), 'dp', axis=1, tiled=True)  32.8 us
    all_to_all x2, waiting for transfers between devices, sent_and_summed(): lax.all_to_all(cut_along(value, dim, length), axis, 0, 0, tiled=True)  30.5 us
    psum x1, waiting for transfers between devices, local(): lax.psum(act_part.astype(jnp.bfloat16), 'mp').astype(jnp.float32)  20.2 us
    psum x1, waiting for transfers between devices, local(): grad_normed = grad_second + lax.psum(back_part, 'mp')  20.1 us
    unnamed x178, local copies, waits for them, and re-layouts  19.1 us
  transfers between devices with their start and end apart: 11, of which 10 were waited for; matrix products, arithmetic and copies ran while one was open for 8% of the time, Pallas kernels for 0%

profile of v1, /device:TPU:0, one launch (start us, length us, event | category | flops | bytes accessed | tf_op | source)
XLA Modules:
  0.0 670.1 jit_solution(15708946535372922440)
XLA Ops:
  7.2 1.8 copy.145
  11.7 8.3 %all-to-all-start = ((s32[16,24,1]{1,2,0:T(1,128)}), s32[16,24,1]{1,2,0:T(1,128)S(1)}, u32[]{:S(2)}, u32[]{:S(2)}) async-start(s32[16,24,1]{1,2,0:T(1,128)} %bitcast), calls=%async_computation | async-start | bytes 16384 | tf_op jit(solution)/shard_map/all_to_all | solution.py:103
  21.8 5.4 all-to-all-done
  28.7 3.5 all-to-all-start.1
  33.1 8.8 %all-to-all-done.1 = bf16[16,24,384]{2,1,0:T(8,128)(2,1)S(1)} async-done(((bf16[16,24,384]{2,1,0:T(8,128)(2,1)}), bf16[16,24,384]{2,1,0:T(8,128)(2,1)S(1)}, u32[]{:S(2)}, u32[]{:S(2)}) %all-to-all-start.1) | async-done | bytes 294944 | tf_op jit(solution)/shard_map/all_to_all | solution.py:109
  42.4 2.2 all_gather.9
  44.6 32.8 %all-gather.3.cloned.1.call-done = bf16[4,768,384]{2,0,1:T(4,128)(2,1)} async-done(((bf16[4,48,384]{2,0,1:T(4,128)(2,1)}), bf16[4,768,384]{2,0,1:T(4,128)(2,1)}) %all-gather.3.cloned.1.call-update) | async-done | bytes 2359312 | tf_op jit(solution)/shard_map/all_gather | solution.py:88
  77.4 4.1 copy.139
  90.5 1.5 fusion.79
  92.1 2.0 convert_element_type.187
  94.8 16.0 %all-reduce.11.cloned.1.call-done = f32[384,768]{1,0:T(8,128)} async-done(((f32[384,768]{1,0:T(8,128)}), f32[384,768]{1,0:T(8,128)}) %all-reduce.11.cloned.1.call-update) | async-done | bytes 1179664 | tf_op jit(solution)/shard_map/psum | solution.py:157
  110.8 2.0 fusion.110
  114.1 102.9 %all-gather.5.cloned.1.call-done = bf16[3,768,1536]{2,1,0:T(8,128)(2,1)} async-done(((bf16[3,48,1536]{2,1,0:T(8,128)(2,1)}), bf16[3,768,1536]{2,1,0:T(8,128)(2,1)}) %all-gather.5.cloned.1.call-update) | async-done | bytes 7077904 | tf_op jit(solution)/shard_map/all_gather | solution.py:89
  217.0 4.8 fusion.4
  225.0 3.8 fusion.31
  230.9 16.0 %all-reduce.13.cloned.1.call-done = f32[384,768]{1,0:T(8,128)} async-done(((f32[384,768]{1,0:T(8,128)}), f32[384,768]{1,0:T(8,128)}) %all-reduce.13.cloned.1.call-update) | async-done | bytes 1179664 | tf_op jit(solution)/shard_map/psum | solution.py:164
  247.0 2.2 fusion.108
  250.5 1.9 multiply_reduce_fusion.3
  252.4 1.7 fusion.107
  254.1 4.5 fusion.58
  260.0 3.0 fusion.40
  264.1 20.1 %all-reduce.15.cloned.1.call-done = f32[384,768]{1,0:T(8,128)} async-done(((f32[384,768]{1,0:T(8,128)}), f32[384,768]{1,0:T(8,128)}) %all-reduce.15.cloned.1.call-update) | async-done | bytes 1179664 | tf_op jit(solution)/shard_map/psum | solution.py:185
  284.2 4.1 multiply_reduce_fusion.4
  290.5 1.5 fusion.46
  297.1 2.8 fusion.44
  299.9 20.2 %all-reduce.17.cloned.1.call-done = bf16[384,768]{1,0:T(8,128)(2,1)} async-done(((bf16[384,768]{1,0:T(8,128)(2,1)}), bf16[384,768]{1,0:T(8,128)(2,1)}) %all-reduce.17.cloned.1.call-update) | async-done | bytes 589840 | tf_op jit(solution)/shard_map/psum | solution.py:232
  320.1 2.4 broadcast_select_fusion
  322.4 1.7 fusion.71
  324.1 6.8 %all-to-all-start.4 = ((f32[16,24,384]{2,1,0:T(8,128)}), f32[16,24,384]{2,1,0:T(8,128)}, u32[]{:S(2)}, u32[]{:S(2)}) async-start(f32[16,24,384]{2,1,0:T(8,128)} %bitcast.52), calls=%async_computation.4 | async-start | bytes 1179648 | tf_op jit(solution)/shard_map/all_to_all | solution.py:241
  331.0 2.5 convert_bitcast_fusion
  333.5 2.8 copy.121
  337.4 1.8 copy.124
  339.3 8.4 %all-to-all-done.4 = f32[16,24,384]{2,1,0:T(8,128)} async-done(((f32[16,24,384]{2,1,0:T(8,128)}), f32[16,24,384]{2,1,0:T(8,128)}, u32[]{:S(2)}, u32[]{:S(2)}) %all-to-all-start.4) | async-done | bytes 589856 | tf_op jit(solution)/shard_map/all_to_all | solution.py:241
  347.7 4.5 all-to-all-start.2
  352.2 6.6 convolution_convert_fusion
  360.2 2.6 fusion.8
  362.9 5.7 maximum_bitcast_fusion
  368.6 30.5 %all-to-all-done.2 = bf16[16,4,48,384]{3,2,1,0:T(8,128)(2,1)S(1)} async-done(((bf16[16,4,48,384]{3,2,1,0:T(8,128)(2,1)}), bf16[16,4,48,384]{3,2,1,0:T(8,128)(2,1)S(1)}, u32[]{:S(2)}, u32[]{:S(2)}) %all-to-all-start.2) | async-done | bytes 2359328 | tf_op jit(solution)/shard_map/all_to_all | solution.py:29
  399.1 10.9 %all-to-all-start.3 = ((bf16[16,3,48,1536]{3,2,1,0:T(8,128)(2,1)}), bf16[16,3,48,1536]{3,2,1,0:T(8,128)(2,1)}, u32[]{:S(2)}, u32[]{:S(2)}) async-start(bf16[16,3,48,1536]{3,2,1,0:T(8,128)(2,1)} %maximum_bitcast_fusion), calls=%async_computation.3 | async-start | bytes 14155776 | tf_op jit(solution)/shard_map/all_to_all | solution.py:29
  410.6 1.9 pad_maximum_fusion.9
  412.5 166.0 %all-reduce.5 = (f32[3]{0:T(128)S(1)}, f32[]{:T(128)}) all-reduce(f32[3]{0:T(128)S(1)} %pad_maximum_fusion.9, f32[]{:T(128)S(6)} %convert_element_type.207), channel_id=1, replica_groups=mesh['dp'=16,'mp'=2] {'dp'}, use_global_device_ids=true, to_apply=%region_23.24 | all-reduce | flops 4 | bytes 32 | tf_op jit(solution)/shard_map/psum | solution.py:173
  581.1 7.9 %multiply_reduce_fusion.2 = (f32[]{:T(128)}, f32[]{:T(128)}, f32[960,384]{1,0:T(8,128)}, f32[960,384]{1,0:T(8,128)}, f32[960,384]{1,0:T(8,128)}) fusion(f32[960,384]{1,0:T(8,128)} %param.28, f32[960,384]{1,0:T(8,128)} %param.29, f32[960,384]{1,0:T(8,128)} %param.30, f32[]{:T(128)S(6)} %div.121, f32[384,384]{1,0:T(8,128)} %bitcast.53, s32[384]{0:T(512)S(1)} %copy-done.77), kind=kOutput, calls=%fused_computation.65 | convolution fusion | flops 1705328640 | bytes 9438732 | tf_op jit(solution)/shard_map/pr,pc->rc/dot_general | solution.py:242
  590.2 1.5 multiply_reduce_fusion.15
  591.7 4.5 convert_reduce_fusion
  596.2 1.6 multiply_reduce_fusion.13
  599.9 52.9 %all-reduce.4 = (f32[4,768]{1,0:T(4,128)}, f32[8]{0:T(128)}, f32[8]{0:T(128)}) all-reduce(f32[4,768]{1,0:T(4,128)} %maximum_multiply_fusion, f32[8]{0:T(128)} %pad_maximum_fusion.11, f32[8]{0:T(128)S(1)} %pad_maximum_fusion.10), channel_id=1, replica_groups=mesh['dp'=16,'mp'=2] {'dp','mp'}, use_global_device_ids=true, to_apply=%region_40.41 | all-reduce | flops 3088 | bytes 24704 | tf_op jit(solution)/shard_map/psum | solution.py:275
  654.8 1.5 multiply_reduce_fusion.16
  660.9 1.9 multiply_subtract_fusion
  (263 shorter events, 46.8 us)
Async XLA Ops:
  7.2 20.1 %copy-start.25 = (f32[960,384]{1,0:T(8,128)S(1)}, f32[960,384]{1,0:T(8,128)}, u32[]{:S(2)}) copy-start(f32[960,384]{1,0:T(8,128)} %param.28) | copy-start | bytes 4423684
  7.2 70.2 %all-gather.3.cloned.1.call-start = ((), (), s32[]{:S(2)}) async-start(), calls=%async_computation.5 | async-start | bytes 2506752 | tf_op jit(solution)/shard_map/all_gather | solution.py:88
  10.1 31.8 %copy-start.62 = (s32[384]{0:T(512)}, s32[384]{0:T(512)S(1)}, u32[]{:S(2)}) copy-start(s32[384]{0:T(512)S(1)} %convert_element_type.170) | copy-start | bytes 4612
  11.7 15.5 %all-to-all-start = ((s32[16,24,1]{1,2,0:T(1,128)}), s32[16,24,1]{1,2,0:T(1,128)S(1)}, u32[]{:S(2)}, u32[]{:S(2)}) async-start(s32[16,24,1]{1,2,0:T(1,128)} %bitcast), calls=%async_computation | async-start | bytes 16384 | tf_op jit(solution)/shard_map/all_to_all | solution.py:103
  20.8 11.5 %copy-start.78 = (s32[384]{0:T(512)S(1)}, s32[384]{0:T(512)}, u32[]{:S(2)}) copy-start(s32[384]{0:T(512)} %param.20) | copy-start | bytes 4612
  27.3 15.0 %copy-start.76 = (s32[384]{0:T(512)}, s32[384]{0:T(512)S(1)}, u32[]{:S(2)}) copy-start(s32[384]{0:T(512)S(1)} %sub.124) | copy-start | bytes 4612
  28.7 13.3 %all-to-all-start.1 = ((bf16[16,24,384]{2,1,0:T(8,128)(2,1)}), bf16[16,24,384]{2,1,0:T(8,128)(2,1)S(1)}, u32[]{:S(2)}, u32[]{:S(2)}) async-start(bf16[16,24,384]{2,1,0:T(8,128)(2,1)} %bitcast.1), calls=%async_computation.1 | async-start | bytes 589824 | tf_op jit(solution)/shard_map/all_to_all | solution.py:109
  32.2 78.6 %all-reduce.11.cloned.1.call-start = ((), (), s32[]{:S(2)}) async-start(), calls=%async_computation.6 | async-start | bytes 2359296 | tf_op jit(solution)/shard_map/psum | solution.py:157
  32.3 49.3 %copy-start.72 = (pred[384]{0:T(512)(128)(4,1)}, pred[384]{0:T(512)(128)(4,1)S(1)}, u32[]{:S(2)}) copy-start(pred[384]{0:T(512)(128)(4,1)S(1)} %broadcast_compare_fusion.1) | copy-start | bytes 1156
  44.6 37.0 %copy-start.6 = (bf16[384,768]{1,0:T(8,128)(2,1)}, bf16[384,768]{1,0:T(8,128)(2,1)S(1)}, u32[]{:S(2)}) copy-start(bf16[384,768]{1,0:T(8,128)(2,1)S(1)} %all_gather.9) | copy-start | bytes 1769476
  92.0 125.0 %all-gather.5.cloned.1.call-start = ((), (), s32[]{:S(2)}) async-start(), calls=%async_computation.7 | async-start | bytes 7520256 | tf_op jit(solution)/shard_map/all_gather | solution.py:89
  94.1 152.8 %all-reduce.13.cloned.1.call-start = ((), (), s32[]{:S(2)}) async-start(), calls=%async_computation.8 | async-start | bytes 2359296 | tf_op jit(solution)/shard_map/psum | solution.py:164
  112.8 134.1 %copy-start.50 = (f32[384]{0:T(512)}, f32[384]{0:T(512)S(1)}, u32[]{:S(2)}) copy-start(f32[384]{0:T(512)S(1)} %broadcast_multiply_fusion.4) | copy-start | bytes 4612
  114.1 107.7 %copy-start.64 = (f32[384]{0:T(512)}, f32[384]{0:T(512)S(1)}, u32[]{:S(2)}) copy-start(f32[384]{0:T(512)S(1)} %multiply_reduce_fusion.11) | copy-start | bytes 4612
  114.1 132.8 %copy-start.56 = (f32[384]{0:T(512)}, f32[384]{0:T(512)S(1)}, u32[]{:S(2)}) copy-start(f32[384]{0:T(512)S(1)} %fusion.90) | copy-start | bytes 4612
  228.8 55.4 %all-reduce.15.cloned.1.call-start = ((), (), s32[]{:S(2)}) async-start(), calls=%async_computation.9 | async-start | bytes 2359296 | tf_op jit(solution)/shard_map/psum | solution.py:185
  230.9 18.6 %copy-start.55 = (f32[768]{0:T(1024)S(1)}, f32[768]{0:T(1024)}, u32[]{:S(2)}) copy-start(f32[768]{0:T(1024)} %get-tuple-element.83) | copy-start | bytes 9220
  249.2 4.9 slice-start
  252.4 7.7 %slice-start.2 = ((s8[7077888]{0:T(1024)(128)(4,1)}), s8[2883584]{0:T(1024)(128)(4,1)S(1)}, s32[]{:S(2)}) async-start(s8[7077888]{0:T(1024)(128)(4,1)} %bitcast.166), calls=%async_computation.13 | async-start | bytes 5767168
  254.0 4.6 copy-start.14
  254.0 4.6 copy-start.75
  254.0 6.0 slice-start.3
  263.1 57.0 %all-reduce.17.cloned.1.call-start = ((), (), s32[]{:S(2)}) async-start(), calls=%async_computation.10 | async-start | bytes 1179648 | tf_op jit(solution)/shard_map/psum | solution.py:232
  297.1 23.0 %copy-start.4 = (f32[384,768]{1,0:T(8,128)S(1)}, f32[384,768]{1,0:T(8,128)}, u32[]{:S(2)}) copy-start(f32[384,768]{1,0:T(8,128)} %copy-done.3) | copy-start | bytes 3538948
  297.1 23.0 %copy-start.61 = (f32[384]{0:T(512)S(1)}, f32[384]{0:T(512)}, u32[]{:S(2)}) copy-start(f32[384]{0:T(512)} %copy-done.60) | copy-start | bytes 4612
  297.1 23.0 %copy-start.74 = (pred[384]{0:T(512)(128)(4,1)S(1)}, pred[384]{0:T(512)(128)(4,1)}, u32[]{:S(2)}) copy-start(pred[384]{0:T(512)(128)(4,1)} %copy-done.72) | copy-start | bytes 1156
  299.9 22.6 %copy-start.63 = (s32[384]{0:T(512)S(1)}, s32[384]{0:T(512)}, u32[]{:S(2)}) copy-start(s32[384]{0:T(512)} %copy-done.62) | copy-start | bytes 4612
  322.4 8.6 %copy-start.8 = (bf16[384,768]{1,0:T(8,128)(2,1)S(1)}, bf16[384,768]{1,0:T(8,128)(2,1)}, u32[]{:S(2)}) copy-start(bf16[384,768]{1,0:T(8,128)(2,1)} %copy-done.6) | copy-start | bytes 1769476
  322.4 8.6 %copy-start.22 = (bf16[384,768]{1,0:T(8,128)(2,1)S(1)}, bf16[384,768]{1,0:T(8,128)(2,1)}, u32[]{:S(2)}) copy-start(bf16[384,768]{1,0:T(8,128)(2,1)} %param.17) | copy-start | bytes 1769476
  322.4 8.6 %copy-start.44 = (bf16[1,384,384]{2,1,0:T(8,128)(2,1)S(1)}, bf16[1,384,384]{2,1,0:T(8,128)(2,1)}, u32[]{:S(2)}) copy-start(bf16[1,384,384]{2,1,0:T(8,128)(2,1)} %copy.117) | copy-start | bytes 884740
  324.1 23.5 %all-to-all-start.4 = ((f32[16,24,384]{2,1,0:T(8,128)}), f32[16,24,384]{2,1,0:T(8,128)}, u32[]{:S(2)}, u32[]{:S(2)}) async-start(f32[16,24,384]{2,1,0:T(8,128)} %bitcast.52), calls=%async_computation.4 | async-start | bytes 1179648 | tf_op jit(solution)/shard_map/all_to_all | solution.py:241
  339.2 13.0 %copy-start.2 = (f32[384,768]{1,0:T(8,128)S(1)}, f32[384,768]{1,0:T(8,128)}, u32[]{:S(2)}) copy-start(f32[384,768]{1,0:T(8,128)} %copy-done) | copy-start | bytes 3538948
  339.2 13.0 %copy-start.52 = (f32[384]{0:T(512)S(1)}, f32[384]{0:T(512)}, u32[]{:S(2)}) copy-start(f32[384]{0:T(512)} %copy-done.50) | copy-start | bytes 4612
  339.3 13.0 %copy-start.58 = (f32[384]{0:T(512)S(1)}, f32[384]{0:T(512)}, u32[]{:S(2)}) copy-start(f32[384]{0:T(512)} %copy-done.56) | copy-start | bytes 4612
  339.3 13.0 %copy-start.69 = (f32[768]{0:T(1024)S(1)}, f32[768]{0:T(1024)}, u32[]{:S(2)}) copy-start(f32[768]{0:T(1024)} %get-tuple-element.85) | copy-start | bytes 9220
  347.7 51.4 %all-to-all-start.2 = ((bf16[16,4,48,384]{3,2,1,0:T(8,128)(2,1)}), bf16[16,4,48,384]{3,2,1,0:T(8,128)(2,1)S(1)}, u32[]{:S(2)}, u32[]{:S(2)}) async-start(bf16[16,4,48,384]{3,2,1,0:T(8,128)(2,1)} %copy.124), calls=%async_computation.2 | async-start | bytes 4718592 | tf_op jit(solution)/shard_map/all_to_all | solution.py:29
  368.5 210.0 %copy-start.71 = (f32[768]{0:T(1024)S(1)}, f32[768]{0:T(1024)}, u32[]{:S(2)}) copy-start(f32[768]{0:T(1024)} %get-tuple-element.73) | copy-start | bytes 9220
  368.5 211.3 %copy-start.70 = (f32[768]{0:T(1024)S(1)}, f32[768]{0:T(1024)}, u32[]{:S(2)}) copy-start(f32[768]{0:T(1024)} %get-tuple-element.80) | copy-start | bytes 9220
  368.6 211.9 %copy-start.68 = (f32[768]{0:T(1024)S(1)}, f32[768]{0:T(1024)}, u32[]{:S(2)}) copy-start(f32[768]{0:T(1024)} %get-tuple-element.71) | copy-start | bytes 9220
  368.6 211.9 %copy-start.67 = (f32[768]{0:T(1024)S(1)}, f32[768]{0:T(1024)}, u32[]{:S(2)}) copy-start(f32[768]{0:T(1024)} %get-tuple-element.77) | copy-start | bytes 9220
  368.6 212.5 %copy-start.77 = (s32[384]{0:T(512)S(1)}, s32[384]{0:T(512)}, u32[]{:S(2)}) copy-start(s32[384]{0:T(512)} %copy-done.76) | copy-start | bytes 4612
  399.1 192.6 %all-to-all-start.3 = ((bf16[16,3,48,1536]{3,2,1,0:T(8,128)(2,1)}), bf16[16,3,48,1536]{3,2,1,0:T(8,128)(2,1)}, u32[]{:S(2)}, u32[]{:S(2)}) async-start(bf16[16,3,48,1536]{3,2,1,0:T(8,128)(2,1)} %maximum_bitcast_fusion), calls=%async_computation.3 | async-start | bytes 14155776 | tf_op jit(solution)/shard_map/all_to_all | solution.py:29
  591.6 66.1 %copy-start.39 = (f32[4,48,384]{2,1,0:T(8,128)}, f32[4,48,384]{2,1,0:T(8,128)S(1)}, u32[]{:S(2)}) copy-start(f32[4,48,384]{2,1,0:T(8,128)S(1)} %get-tuple-element.100) | copy-start | bytes 884740
  591.6 66.1 %copy-start.40 = (f32[4,48,384]{2,1,0:T(8,128)}, f32[4,48,384]{2,1,0:T(8,128)S(1)}, u32[]{:S(2)}) copy-start(f32[4,48,384]{2,1,0:T(8,128)S(1)} %get-tuple-element.101) | copy-start | bytes 884740
  591.7 4.5 copy-start.41
  596.2 58.6 %copy-start.49 = (f32[4,768]{1,0:T(4,128)S(1)}, f32[4,768]{1,0:T(4,128)}, u32[]{:S(2)}) copy-start(f32[4,768]{1,0:T(4,128)} %param.31) | copy-start | bytes 36868
  597.9 62.1 %copy-start.16 = (f32[3,48,1536]{2,1,0:T(8,128)}, f32[3,48,1536]{2,1,0:T(8,128)S(1)}, u32[]{:S(2)}) copy-start(f32[3,48,1536]{2,1,0:T(8,128)S(1)} %get-tuple-element.103) | copy-start | bytes 2654212
  597.9 62.1 %copy-start.17 = (f32[3,48,1536]{2,1,0:T(8,128)}, f32[3,48,1536]{2,1,0:T(8,128)S(1)}, u32[]{:S(2)}) copy-start(f32[3,48,1536]{2,1,0:T(8,128)S(1)} %get-tuple-element.104) | copy-start | bytes 2654212
  (51 other events, 106.9 us)
Sparse Core Ops, SparseCore 0:
  11.4 65.9 all-gather.2
  92.2 18.6 all-reduce.10
  114.4 102.5 all-gather.4
  228.9 17.9 all-reduce.12
  263.2 20.9 all-reduce.14
  300.0 20.0 all-reduce.16

commit v2 on v1

--- a/solution.py
+++ b/solution.py
@@ -3,6 +3,8 @@
 import jax
 import jax.numpy as jnp
 from jax import lax
+from jax.experimental import pallas as pl
+from jax.experimental.pallas import tpu as pltpu
 from jax.sharding import PartitionSpec as P
 
 HEADS = 12
@@ -54,6 +56,332 @@
 
 def gelu_tanh(values):
     return jax.nn.gelu(values, approximate=True)
+
+MESH_ID = pl.DeviceIdType.MESH
+PLANES = 4
+CUT = 384
+
+
+def here():
+    place = lax.axis_index("dp")
+    return place // 4, (place // 2) % 2, place % 2, lax.axis_index("mp")
+
+
+def device_at(z, y, x, core):
+    return (z * 4 + y * 2 + x, core)
+
+
+def meet(peers):
+    barrier = pltpu.get_barrier_semaphore()
+    for peer in peers:
+        pl.semaphore_signal(barrier, inc=1, device_id=peer, device_id_type=MESH_ID)
+    pl.semaphore_wait(barrier, len(peers))
+
+
+def chip_peers():
+    z, y, x, core = here()
+    peers = [device_at((z + k) % PLANES, y, x, core) for k in range(1, PLANES)]
+    return peers + [device_at(z, 1 - y, x, core), device_at(z, y, 1 - x, core)]
+
+
+class Gather:
+    def __init__(self, held, z_send, z_recv, near_send, near_recv):
+        self.held, self.z_send, self.z_recv = held, z_send, z_recv
+        self.near_send, self.near_recv = near_send, near_recv
+
+    def along_z(self, c, k):
+        z, y, x, core = here()
+        block = self.held.at[c, z, y, x]
+        return pltpu.make_async_remote_copy(
+            src_ref=block,
+            dst_ref=block,
+            send_sem=self.z_send.at[c, k - 1],
+            recv_sem=self.z_recv.at[c, k - 1],
+            device_id=device_at((z + k) % PLANES, y, x, core),
+            device_id_type=MESH_ID,
+        )
+
+    def near(self, c, flip, stage):
+        z, y, x, core = here()
+        first_y = flip == 0
+        go_y = first_y if stage == 0 else not first_y
+        if stage == 0:
+            block = self.held.at[c, :, y, x]
+        elif go_y:
+            block = self.held.at[c, :, y]
+        else:
+            block = self.held.at[c, :, :, x]
+        target = device_at(z, 1 - y, x, core) if go_y else device_at(z, y, 1 - x, core)
+        return pltpu.make_async_remote_copy(
+            src_ref=block,
+            dst_ref=block,
+            send_sem=self.near_send.at[stage, c],
+            recv_sem=self.near_recv.at[stage, c],
+            device_id=target,
+            device_id_type=MESH_ID,
+        )
+
+    def start_z(self, pair):
+        for flip in range(2):
+            for k in range(1, PLANES):
+                self.along_z(2 * pair + flip, k).start()
+
+    def start_near(self, pair, stage):
+        for flip in range(2):
+            self.near(2 * pair + flip, flip, stage).start()
+
+    def wait_z(self, pair):
+        for flip in range(2):
+            for k in range(1, PLANES):
+                self.along_z(2 * pair + flip, k).wait()
+
+    def wait_near(self, pair, stage):
+        for flip in range(2):
+            self.near(2 * pair + flip, flip, stage).wait()
+
+
+def gather_kernel(chunks, attention_ref, geglu_ref, held, z_send, z_recv, near_send, near_recv):
+    z, y, x, _ = here()
+    meet(chip_peers())
+    wide = geglu_ref.shape[2] // CUT
+    for c in range(chunks):
+        if c < 4:
+            shard = attention_ref[c]
+        else:
+            at = (c - 4) % wide * CUT
+            shard = geglu_ref[(c - 4) // wide, :, at : at + CUT]
+        held[c, z, y, x] = shard.astype(held.dtype)
+    ring = Gather(held, z_send, z_recv, near_send, near_recv)
+    pairs = chunks // 2
+    ring.start_z(0)
+    ring.start_z(1)
+    ring.wait_z(0)
+    ring.start_near(0, 0)
+
+    @pl.loop(0, pairs)
+    def _(pair):
+        ring.wait_near(pair, 0)
+        ring.start_near(pair, 1)
+
+        @pl.when(pair + 1 < pairs)
+        def _():
+            ring.wait_z(pair + 1)
+            ring.start_near(pair + 1, 0)
+
+        @pl.when(pair + 2 < pairs)
+        def _():
+            ring.start_z(pair + 2)
+
+        @pl.when(pair > 0)
+        def _():
+            ring.wait_near(pair - 1, 1)
+
+    ring.wait_near(pairs - 1, 1)
+
+
+def gather_weights(attention_master, geglu_master):
+    rows = attention_master.shape[1]
+    chunks = 4 + 3 * geglu_master.shape[2] // CUT
+    held = pl.pallas_call(
+        lambda *refs: gather_kernel(chunks, *refs),
+        out_shape=jax.ShapeDtypeStruct((chunks, PLANES, 2, 2, rows, CUT), jnp.bfloat16),
+        in_specs=[pl.BlockSpec(memory_space=pltpu.VMEM)] * 2,
+        out_specs=pl.BlockSpec(memory_space=pltpu.VMEM),
+        scratch_shapes=[
+            pltpu.SemaphoreType.DMA((chunks, PLANES - 1)),
+            pltpu.SemaphoreType.DMA((chunks, PLANES - 1)),
+            pltpu.SemaphoreType.DMA((2, chunks)),
+            pltpu.SemaphoreType.DMA((2, chunks)),
+        ],
+        compiler_params=pltpu.CompilerParams(
+            collective_id=0, has_side_effects=True, vmem_limit_bytes=32 << 20
+        ),
+        name="gather_weights",
+    )(attention_master, geglu_master)
+    return held.reshape(chunks, rows * PLANES * 4, CUT)
+
+
+class Scatter:
+    def __init__(self, grads, far_got, mid_got, z_got, z_send, z_recv, near_send, near_recv):
+        self.grads, self.far_got, self.mid_got, self.z_got = grads, far_got, mid_got, z_got
+        self.z_send, self.z_recv = z_send, z_recv
+        self.near_send, self.near_recv = near_send, near_recv
+
+    def near(self, c, flip, stage):
+        z, y, x, core = here()
+        first_x = flip == 0
+        go_x = first_x if stage == 0 else not first_x
+        if stage == 0:
+            block = self.grads.at[c, :, :, 1 - x] if go_x else self.grads.at[c, :, 1 - y]
+            got = self.far_got.at[c]
+        else:
+            block = self.grads.at[c, :, y, 1 - x] if go_x else self.grads.at[c, :, 1 - y, x]
+            got = self.mid_got.at[c]
+        target = device_at(z, y, 1 - x, core) if go_x else device_at(z, 1 - y, x, core)
+        return pltpu.make_async_remote_copy(
+            src_ref=block,
+            dst_ref=got,
+            send_sem=self.near_send.at[stage, c],
+            recv_sem=self.near_recv.at[stage, c],
+            device_id=target,
+            device_id_type=MESH_ID,
+        )
+
+    def along_z(self, c, k):
+        z, y, x, core = here()
+        to = (z + k) % PLANES
+        return pltpu.make_async_remote_copy(
+            src_ref=self.grads.at[c, to, y, x],
+            dst_ref=self.z_got.at[c, k - 1],
+            send_sem=self.z_send.at[c, k - 1],
+            recv_sem=self.z_recv.at[c, k - 1],
+            device_id=device_at(to, y, x, core),
+            device_id_type=MESH_ID,
+        )
+
+    def start_near(self, pair, stage):
+        for flip in range(2):
+            self.near(2 * pair + flip, flip, stage).start()
+
+    def start_z(self, pair):
+        for flip in range(2):
+            for k in range(1, PLANES):
+                self.along_z(2 * pair + flip, k).start()
+
+    def add_near(self, pair, stage):
+        z, y, x, core = here()
+        for flip in range(2):
+            c = 2 * pair + flip
+            self.near(c, flip, stage).wait()
+            for plane in range(PLANES):
+                if stage == 1:
+                    mine, got = [(self.grads.at[c, plane, y, x])], [self.mid_got.at[c, plane]]
+                else:
+                    mine = [
+                        self.grads.at[c, plane, k, x] if flip == 0 else self.grads.at[c, plane, y, k]
+                        for k in range(2)
+                    ]
+                    got = [self.far_got.at[c, plane, k] for k in range(2)]
+                for own, other in zip(mine, got):
+                    own[...] = (
+                        own[...].astype(jnp.float32) + other[...].astype(jnp.float32)
+                    ).astype(own.dtype)
+
+    def finish(self, pair, write):
+        z, y, x, core = here()
+        for flip in range(2):
+            c = 2 * pair + flip
+            total = self.grads[c, z, y, x].astype(jnp.float32)
+            for k in range(1, PLANES):
+                self.along_z(c, k).wait()
+                total = total + self.z_got[c, k - 1].astype(jnp.float32)
+            write(c, total)
+
+
+def scatter_kernel(chunks, local_ref, out_ref, grads, far_got, mid_got, z_got, *sems):
+    meet(chip_peers())
+    ring = Scatter(grads, far_got, mid_got, z_got, *sems[:4])
+    pairs = chunks // 2
+
+    def fetch(pair):
+        part = pl.ds(2 * pair, 2)
+        return pltpu.make_async_copy(local_ref.at[part], grads.at[part], sems[4].at[pair])
+
+    def write(c, total):
+        out_ref[c] = total
+
+    for pair in range(2):
+        fetch(pair).start()
+    fetch(0).wait()
+    ring.start_near(0, 0)
+
+    @pl.loop(0, pairs + 2)
+    def _(pair):
+        @pl.when(pair + 2 < pairs)
+        def _():
+            fetch(pair + 2).start()
+
+        @pl.when(pair + 1 < pairs)
+        def _():
+            fetch(pair + 1).wait()
+            ring.start_near(pair + 1, 0)
+
+        @pl.when(pair < pairs)
+        def _():
+            ring.add_near(pair, 0)
+            ring.start_near(pair, 1)
+
+        @pl.when((pair > 0) & (pair <= pairs))
+        def _():
+            ring.add_near(pair - 1, 1)
+            ring.start_z(pair - 1)
+
+        @pl.when(pair > 1)
+        def _():
+            ring.finish(pair - 2, write)
+
+
+def scatter_grads(local):
+    chunks, depth, _ = local.shape
+    rows = depth // (PLANES * 4)
+    local = local.reshape(chunks, PLANES, 2, 2, rows, CUT)
+    half = jnp.bfloat16
+    return pl.pallas_call(
+        lambda *refs: scatter_kernel(chunks, *refs),
+        out_shape=jax.ShapeDtypeStruct((chunks, rows, CUT), jnp.float32),
+        in_specs=[pl.BlockSpec(memory_space=pl.ANY)],
+        out_specs=pl.BlockSpec(memory_space=pltpu.VMEM),
+        scratch_shapes=[
+            pltpu.VMEM((chunks, PLANES, 2, 2, rows, CUT), half),
+            pltpu.VMEM((chunks, PLANES, 2, rows, CUT), half),
+            pltpu.VMEM((chunks, PLANES, rows, CUT), half),
+            pltpu.VMEM((chunks, PLANES - 1, rows, CUT), half),
+            pltpu.SemaphoreType.DMA((chunks, PLANES - 1)),
+            pltpu.SemaphoreType.DMA((chunks, PLANES - 1)),
+            pltpu.SemaphoreType.DMA((2, chunks)),
+            pltpu.SemaphoreType.DMA((2, chunks)),
+            pltpu.SemaphoreType.DMA((chunks // 2,)),
+        ],
+        compiler_params=pltpu.CompilerParams(
+            collective_id=1, has_side_effects=True, vmem_limit_bytes=40 << 20
+        ),
+        name="scatter_grads",
+    )(local)
+
+
+def core_sum_kernel(part_ref, out_ref, got, send, recv):
+    z, y, x, core = here()
+    other = device_at(z, y, x, 1 - core)
+    meet([other])
+    copy = pltpu.make_async_remote_copy(
+        src_ref=part_ref,
+        dst_ref=got,
+        send_sem=send,
+        recv_sem=recv,
+        device_id=other,
+        device_id_type=MESH_ID,
+    )
+    copy.start()
+    copy.wait()
+    out_ref[...] = (part_ref[...].astype(jnp.float32) + got[...].astype(jnp.float32)).astype(
+        out_ref.dtype
+    )
+
+
+def core_sum(part, number):
+    return pl.pallas_call(
+        core_sum_kernel,
+        out_shape=jax.ShapeDtypeStruct(part.shape, jnp.float32),
+        in_specs=[pl.BlockSpec(memory_space=pltpu.VMEM)],
+        out_specs=pl.BlockSpec(memory_space=pltpu.VMEM),
+        scratch_shapes=[
+            pltpu.VMEM(part.shape, part.dtype),
+            pltpu.SemaphoreType.DMA,
+            pltpu.SemaphoreType.DMA,
+        ],
+        compiler_params=pltpu.CompilerParams(collective_id=number, has_side_effects=True),
+        name="core_sum_%d" % number,
+    )(part)
 
 
 def local(
@@ -84,11 +412,24 @@
     block_len = min(tokens_here, 512)
     attn_scale = 1.0 / math.sqrt(head_dim)
     column_count = embed_master.shape[1]
-    attn_low, geglu_low = (
-        lax.all_gather(attention_master.astype(half_type), "dp", axis=1, tiled=True),
-        lax.all_gather(geglu_master.astype(half_type), "dp", axis=1, tiled=True),
-    )
     owners = lax.axis_size("dp")
+    own_comm = owners == 16 and attention_master.shape[1:] == (48, CUT)
+    if own_comm:
+        held = gather_weights(attention_master, geglu_master)
+        attn_low = held[:4]
+        wide = geglu_master.shape[2] // CUT
+        geglu_low = jnp.concatenate([held[4 + k :: wide] for k in range(wide)], axis=2)
+    else:
+        attn_low, geglu_low = (
+            lax.all_gather(attention_master.astype(half_type), "dp", axis=1, tiled=True),
+            lax.all_gather(geglu_master.astype(half_type), "dp", axis=1, tiled=True),
+        )
+
+    def mp_sum(value, number):
+        if own_comm:
+            return core_sum(value, number)
+        return lax.psum(value, "mp").astype(full_type)
+
     owner_rows = embed_master.shape[0]
     per_owner = tokens_here // owners
     owner_low = jnp.arange(owners, dtype=jnp.int32)[:, None] * owner_rows
@@ -154,14 +495,14 @@
     context_blocks, lse_blocks = lax.map(forward_block, starts)
     context = context_blocks.reshape(tokens_here, local_heads * head_dim)
     attn_part = jnp.einsum("tc,dc->td", context, attn_low[3], preferred_element_type=full_type)
-    attn_out = lax.psum(attn_part, "mp")
+    attn_out = mp_sum(attn_part, 2)
     normed_one, first_back = jax.vjp(norm_pair, hidden_in + attn_out, norms_master[0:2])
     normed_low = normed_one.astype(half_type)
     gate_up = jnp.einsum("td,kdf->ktf", normed_low, geglu_low[:2], preferred_element_type=full_type)
     gelu_val, gelu_back = jax.vjp(gelu_tanh, gate_up[0])
     inner_act = (gelu_val * gate_up[1]).astype(half_type)
     geglu_part = jnp.einsum("tf,df->td", inner_act, geglu_low[2], preferred_element_type=full_type)
-    geglu_out = lax.psum(geglu_part, "mp")
+    geglu_out = mp_sum(geglu_part, 2)
     result, second_back = jax.vjp(norm_pair, normed_one + geglu_out, norms_master[2:4])
     squares = jnp.stack(
         [
@@ -182,7 +523,7 @@
     gu_grad = jnp.einsum("td,ktf->kdf", normed_low, grad_gu, preferred_element_type=full_type)
     geglu_local = jnp.concatenate([gu_grad, down_grad[None]], axis=0)
     back_part = jnp.einsum("ktf,kdf->td", grad_gu, geglu_low[:2], preferred_element_type=full_type)
-    grad_normed = grad_second + lax.psum(back_part, "mp")
+    grad_normed = grad_second + mp_sum(back_part, 2)
     grad_first_in, norm_grad_one = first_back(grad_normed)
     grad_attn = grad_first_in.astype(half_type)
     grad_context = jnp.einsum(
@@ -229,7 +570,7 @@
     )
     qkv_grad = jnp.einsum("td,ktc->kdc", act_low, grad_qkv, preferred_element_type=full_type)
     act_part = jnp.einsum("ktc,kdc->td", grad_qkv, attn_low[:3], preferred_element_type=full_type)
-    grad_in = grad_first_in + lax.psum(act_part.astype(jnp.bfloat16), "mp").astype(jnp.float32)
+    grad_in = grad_first_in + mp_sum(act_part.astype(jnp.bfloat16), 3)
     input_grad = jnp.where(is_masked, 0.0, grad_in)
     attention_local = jnp.concatenate([qkv_grad, out_grad[None]], axis=0)
     own_columns = lax.dynamic_slice_in_dim(
@@ -240,10 +581,19 @@
     sorted_grads = jnp.dot(moves.astype(full_type), picked, precision=highest)
     got_grads = lax.all_to_all(sorted_grads, "dp", 0, 0, tiled=True)
     embed_summed = jnp.einsum("pr,pc->rc", hits.astype(full_type), got_grads, precision=highest)
-    attention_summed, geglu_summed = (
-        sent_and_summed(attention_local.astype(jnp.bfloat16), "dp", 1),
-        sent_and_summed(geglu_local.astype(jnp.bfloat16), "dp", 1),
-    )
+    if own_comm:
+        geglu_cut = geglu_local.astype(half_type).reshape(3, width, wide, CUT)
+        geglu_cut = jnp.moveaxis(geglu_cut, 2, 1).reshape(3 * wide, width, CUT)
+        summed = scatter_grads(
+            jnp.concatenate([attention_local.astype(half_type), geglu_cut], axis=0)
+        )
+        attention_summed = summed[:4]
+        geglu_summed = jnp.concatenate([summed[4 + k :: wide] for k in range(wide)], axis=2)
+    else:
+        attention_summed, geglu_summed = (
+            sent_and_summed(attention_local.astype(jnp.bfloat16), "dp", 1),
+            sent_and_summed(geglu_local.astype(jnp.bfloat16), "dp", 1),
+        )
     inverse_count = 1.0 / count_total
     attention_grad = attention_summed * inverse_count
     geglu_grad = geglu_summed * inverse_count

time: 680 us -> 479 us (0.70)
  waiting for transfers between devices: 261 us -> 0.01 us
  Pallas kernels: 0 us -> 214 us
  blocking collectives: 221 us -> 82.5 us
  starting transfers between devices: 34.7 us -> 19.6 us
  between operations: 18.3 us -> 4.74 us
  local copies, waits for them, and re-layouts: 30.1 us -> 43.1 us
    pallas_call x0 -> x6, Pallas kernels: none -> 214 us  [the longest x1 99.9 us: gather_weights(): pl.pallas_call(lambda *refs: gather_kernel(chunks, *refs), out_shape=jax....]
    all_gather x2 -> x0, waiting for transfers between devices: 136 us -> none  [the longest x1 103 us: local(): lax.all_gather(geglu_master.astype(half_type), 'dp', axis=1, tiled=True)]
    psum x1, blocking collectives: 166 us -> 42.6 us  [local(): count_total, square_total = lax.psum((token_count, squares), 'dp')]
    psum x4 -> x0, waiting for transfers between devices: 72.4 us -> none  [the longest x1 20.2 us: local(): lax.psum(act_part.astype(jnp.bfloat16), 'mp').astype(jnp.float32)]
    all_to_all x2 -> x0, waiting for transfers between devices: 30.5 us -> none  [sent_and_summed(): lax.all_to_all(cut_along(value, dim, length), axis, 0, 0, tiled=True)]
    psum x1, blocking collectives: 52.9 us -> 37.4 us  [local(): lax.psum((weight_squares, update_squares, norms_local * 0.5), ('dp', 'mp'))]
    all_to_all x2 -> x0, starting transfers between devices: 15.4 us -> none  [sent_and_summed(): lax.all_to_all(cut_along(value, dim, length), axis, 0, 0, tiled=True)]
    all_to_all x1, waiting for transfers between devices: 8.82 us -> 0.01 us  [local(): got_rows = lax.all_to_all(sent_rows, 'dp', 0, 0, tiled=True)]
  transfers between devices with their start and end apart: 11 -> 3, of which waited for: 10 -> 0; matrix products, arithmetic and copies ran while one was open for 8% -> 8% of each run, Pallas kernels for 0% -> 21%
where the time goes in v2:
time: 479 us; the launch traced here: 471 us
  Pallas kernels  214 us (45%)
  blocking collectives  82.5 us (17%)
  matrix products  54 us (11%)
  other arithmetic  53.2 us (11%)
  local copies, waits for them, and re-layouts  43.1 us (9%)
  starting transfers between devices  19.6 us (4%)
    pallas_call x1, Pallas kernels, gather_weights(): pl.pallas_call(lambda *refs: gather_kernel(chunks, *refs), out_shape=jax....  99.9 us
    pallas_call x1, Pallas kernels, scatter_grads(): pl.pallas_call(lambda *refs: scatter_kernel(chunks, *refs), out_shape=jax...  93.6 us
    psum x1, blocking collectives, local(): count_total, square_total = lax.psum((token_count, squares), 'dp')  42.6 us
    psum x1, blocking collectives, local(): lax.psum((weight_squares, update_squares, norms_local * 0.5), ('dp', 'mp'))  37.4 us
    unnamed x200, local copies, waits for them, and re-layouts  24.7 us
    pallas_call x4, Pallas kernels, core_sum(): pl.pallas_call(core_sum_kernel, out_shape=jax.ShapeDtypeStruct(part.shape...  20.2 us
  transfers between devices with their start and end apart: 3, of which 0 were waited for; matrix products, arithmetic and copies ran while one was open for 8% of the time, Pallas kernels for 21%

profile of v2, /device:TPU:0, one launch (start us, length us, event | category | flops | bytes accessed | tf_op | source)
XLA Modules:
  0.0 470.9 jit_solution(9865586986326092536)
XLA Ops:
  3.2 8.3 %all-to-all-start = ((s32[16,24,1]{1,2,0:T(1,128)}), s32[16,24,1]{1,2,0:T(1,128)S(1)}, u32[]{:S(2)}, u32[]{:S(2)}) async-start(s32[16,24,1]{1,2,0:T(1,128)} %bitcast), calls=%async_computation | async-start | bytes 16384 | tf_op jit(solution)/shard_map/all_to_all | solution.py:444
  18.5 99.9 %gather_weights.1 = bf16[16,4,2,2,48,384]{5,4,3,2,1,0:T(8,128)(2,1)S(1)} custom-call(f32[4,48,384]{2,1,0:T(8,128)S(1)} %copy-done.3, f32[3,48,1536]{2,1,0:T(8,128)S(1)} %copy-done.1), custom_call_target="tpu_custom_call" | custom-call | tf_op jit(solution)/shard_map/gather_weights/pallas_call | solution.py:185
  118.5 2.5 fusion.138
  121.0 2.7 copy-done
  127.0 6.1 %all-to-all-start.1 = ((bf16[16,24,384]{2,1,0:T(8,128)(2,1)}), bf16[16,24,384]{2,1,0:T(8,128)(2,1)}, u32[]{:S(2)}, u32[]{:S(2)}) async-start(bf16[16,24,384]{2,1,0:T(8,128)(2,1)} %bitcast.1), calls=%async_computation.1 | async-start | bytes 589824 | tf_op jit(solution)/shard_map/all_to_all | solution.py:450
  133.1 2.9 slice.119
  136.0 1.9 slice.124
  139.6 3.1 copy.142
  142.7 4.2 copy.143
  146.9 3.9 copy.144
  151.5 4.9 %maximum_bitcast_fusion = bf16[768,1536]{0,1:T(8,128)(2,1)} fusion(bf16[3,768,384]{1,2,0:T(8,128)(2,1)} %copy.144, bf16[3,768,384]{1,2,0:T(8,128)(2,1)} %copy.143, bf16[3,768,384]{1,2,0:T(8,128)(2,1)S(1)} %copy.142, bf16[3,768,384]{1,2,0:T(8,128)(2,1)S(1)} %copy.141), kind=kLoop, calls=%fused_computation.56 | loop fusion | flops 9437184 | bytes 9437184 | tf_op jit(solution)/shard_map/squeeze | solution.py:504
  157.8 2.4 all_gather.3
  160.2 3.0 fusion.56
  167.8 1.5 fusion.142.part_ref
  169.4 5.3 %core_sum_2.3 = f32[384,768]{1,0:T(8,128)} custom-call(f32[384,768]{1,0:T(8,128)} %fusion.142.part_ref), custom_call_target="tpu_custom_call" | custom-call | tf_op jit(solution)/shard_map/core_sum_2/pallas_call | solution.py:372
  174.7 2.1 fusion.136
  177.8 6.0 %fusion.17 = f32[2,384,1536]{1,2,0:T(8,128)S(1)} fusion(bf16[3,768,384]{1,2,0:T(8,128)(2,1)} %copy.144, bf16[3,768,384]{1,2,0:T(8,128)(2,1)} %copy.143, bf16[3,768,384]{1,2,0:T(8,128)(2,1)S(1)} %copy-done.17, bf16[3,768,384]{1,2,0:T(8,128)(2,1)S(1)} %copy-done.14, f32[384,768]{1,0:T(8,128)S(1)} %get-tuple-element.118, f32[768]{0:T(1024)S(1)} %copy-done.71, ...), kind=kOutput, calls=%fused_computation.26 | convolution fusion | flops 1841725440 | bytes 12985344 | tf_op jit(solution)/shard_map/td,kdf->ktf/dot_general | solution.py:501
  183.9 2.1 copy-done.88
  186.0 2.4 fusion.68.part_ref
  188.4 5.3 %core_sum_2.4 = f32[384,768]{1,0:T(8,128)} custom-call(f32[384,768]{1,0:T(8,128)} %fusion.68.part_ref), custom_call_target="tpu_custom_call" | custom-call | tf_op jit(solution)/shard_map/core_sum_2/pallas_call | solution.py:372
  193.8 2.2 fusion.134
  196.6 2.0 multiply_reduce_fusion.3
  198.6 1.7 fusion.133
  200.4 3.5 fusion.76
  205.3 3.1 fusion.53.part_ref
  208.4 5.3 %core_sum_2.5 = f32[384,768]{1,0:T(8,128)} custom-call(f32[384,768]{1,0:T(8,128)} %fusion.53.part_ref), custom_call_target="tpu_custom_call" | custom-call | tf_op jit(solution)/shard_map/core_sum_2/pallas_call | solution.py:372
  213.7 3.3 multiply_reduce_fusion.4
  223.3 1.5 fusion.59
  228.4 2.5 convert_bitcast_fusion.1
  231.0 1.8 fusion.57.part_ref
  232.8 5.0 %convert_bitcast_fusion = bf16[2,768,1536]{2,1,0:T(8,128)(2,1)} fusion(bf16[1,384,1536]{1,2,0:T(8,128)(2,1)S(1)} %copy-done.93, bf16[1,384,1536]{1,2,0:T(8,128)(2,1)S(1)} %copy-done.91, f32[384,768]{1,0:T(8,128)S(1)} %copy-done.7, f32[768]{0:T(1024)S(1)} %copy-done.72, f32[768]{0:T(1024)S(1)} %get-tuple-element.86, f32[384]{0:T(512)S(1)} %copy-done.61, ...), kind=kOutput, calls=%fused_computation.25 | convolution fusion | flops 1816952832 | bytes 8266752 | tf_op jit(solution)/shard_map/td,ktf->kdf/dot_general | solution.py:523
  237.8 2.1 fusion.21
  240.0 3.9 copy.122
  243.8 4.4 core_sum_3.1
  248.2 3.1 broadcast_select_fusion
  252.7 1.6 fusion.58
  254.4 2.4 fusion.45
  259.4 93.6 %scatter_grads.1 = f32[16,48,384]{2,1,0:T(8,128)S(1)} custom-call(bf16[16,4,2,2,48,384]{5,4,3,2,1,0:T(8,128)(2,1)S(1)} %pad_maximum_fusion.refs_0_), custom_call_target="tpu_custom_call" | custom-call | tf_op jit(solution)/shard_map/scatter_grads/pallas_call | solution.py:329
  353.1 1.7 fusion.89
  354.8 5.2 %all-to-all-start.2 = ((f32[16,24,384]{2,1,0:T(8,128)}), f32[16,24,384]{2,1,0:T(8,128)}, u32[]{:S(2)}, u32[]{:S(2)}) async-start(f32[16,24,384]{2,1,0:T(8,128)} %bitcast.48), calls=%async_computation.2 | async-start | bytes 1179648 | tf_op jit(solution)/shard_map/all_to_all | solution.py:582
  360.1 2.0 pad_maximum_fusion.11
  362.1 42.6 %all-reduce.5 = (f32[3]{0:T(128)S(1)}, f32[]{:T(128)}) all-reduce(f32[3]{0:T(128)S(1)} %pad_maximum_fusion.11, f32[]{:T(128)S(6)} %convert_element_type.189), channel_id=1, replica_groups=mesh['dp'=16,'mp'=2] {'dp'}, use_global_device_ids=true, to_apply=%region_19.20 | all-reduce | flops 4 | bytes 32 | tf_op jit(solution)/shard_map/psum | solution.py:514
  407.4 1.5 multiply_reduce_fusion.15
  409.1 2.2 multiply_reduce_fusion.13
  411.3 8.6 %multiply_reduce_fusion.2 = (f32[]{:T(128)}, f32[]{:T(128)}, f32[960,384]{1,0:T(8,128)}, f32[960,384]{1,0:T(8,128)}, f32[960,384]{1,0:T(8,128)}) fusion(f32[960,384]{1,0:T(8,128)} %param.28, f32[960,384]{1,0:T(8,128)} %param.29, f32[960,384]{1,0:T(8,128)} %param.30, f32[]{:T(128)S(6)} %div.121, f32[384,384]{1,0:T(8,128)} %bitcast.49, s32[384]{0:T(512)S(1)} %copy-done.83), kind=kOutput, calls=%fused_computation.84 | convolution fusion | flops 1705328640 | bytes 9438732 | tf_op jit(solution)/shard_map/pr,pc->rc/dot_general | solution.py:583
  421.9 37.4 %all-reduce.4 = (f32[4,768]{1,0:T(4,128)}, f32[8]{0:T(128)}, f32[8]{0:T(128)}) all-reduce(f32[4,768]{1,0:T(4,128)} %maximum_multiply_fusion.1, f32[8]{0:T(128)} %pad_maximum_fusion.13, f32[8]{0:T(128)S(1)} %pad_maximum_fusion.12), channel_id=1, replica_groups=mesh['dp'=16,'mp'=2] {'dp','mp'}, use_global_device_ids=true, to_apply=%region_34.35 | all-reduce | flops 3088 | bytes 24704 | tf_op jit(solution)/shard_map/psum | solution.py:625
  460.7 1.5 multiply_reduce_fusion.16
  464.2 4.1 multiply_subtract_fusion
  (268 shorter events, 45.8 us)
Async XLA Ops:
  1.7 154.8 %copy-start.65 = (s32[384]{0:T(512)}, s32[384]{0:T(512)S(1)}, u32[]{:S(2)}) copy-start(s32[384]{0:T(512)S(1)} %convert_element_type.155) | copy-start | bytes 4612
  3.2 122.3 %all-to-all-start = ((s32[16,24,1]{1,2,0:T(1,128)}), s32[16,24,1]{1,2,0:T(1,128)S(1)}, u32[]{:S(2)}, u32[]{:S(2)}) async-start(s32[16,24,1]{1,2,0:T(1,128)} %bitcast), calls=%async_computation | async-start | bytes 16384 | tf_op jit(solution)/shard_map/all_to_all | solution.py:444
  118.4 5.3 %copy-start = (bf16[16,4,2,2,48,384]{5,4,3,2,1,0:T(8,128)(2,1)}, bf16[16,4,2,2,48,384]{5,4,3,2,1,0:T(8,128)(2,1)S(1)}, u32[]{:S(2)}) copy-start(bf16[16,4,2,2,48,384]{5,4,3,2,1,0:T(8,128)(2,1)S(1)} %gather_weights.1) | copy-start | bytes 28311556
  118.4 5.3 %copy-start.53 = (f32[4,768]{1,0:T(4,128)S(1)}, f32[4,768]{1,0:T(4,128)}, u32[]{:S(2)}) copy-start(f32[4,768]{1,0:T(4,128)} %param.31) | copy-start | bytes 36868
  118.4 7.2 %copy-start.37 = (f32[960,384]{1,0:T(8,128)S(1)}, f32[960,384]{1,0:T(8,128)}, u32[]{:S(2)}) copy-start(f32[960,384]{1,0:T(8,128)} %param.28) | copy-start | bytes 4423684
  125.7 10.3 %copy-start.82 = (s32[384]{0:T(512)}, s32[384]{0:T(512)S(1)}, u32[]{:S(2)}) copy-start(s32[384]{0:T(512)S(1)} %sub.124) | copy-start | bytes 4612
  127.0 29.4 %all-to-all-start.1 = ((bf16[16,24,384]{2,1,0:T(8,128)(2,1)}), bf16[16,24,384]{2,1,0:T(8,128)(2,1)}, u32[]{:S(2)}, u32[]{:S(2)}) async-start(bf16[16,24,384]{2,1,0:T(8,128)(2,1)} %bitcast.1), calls=%async_computation.1 | async-start | bytes 589824 | tf_op jit(solution)/shard_map/all_to_all | solution.py:450
  139.6 12.0 %copy-start.13 = (bf16[3,768,384]{1,2,0:T(8,128)(2,1)}, bf16[3,768,384]{1,2,0:T(8,128)(2,1)S(1)}, u32[]{:S(2)}) copy-start(bf16[3,768,384]{1,2,0:T(8,128)(2,1)S(1)} %copy.141) | copy-start | bytes 5308420
  142.7 8.9 %copy-start.16 = (bf16[3,768,384]{1,2,0:T(8,128)(2,1)}, bf16[3,768,384]{1,2,0:T(8,128)(2,1)S(1)}, u32[]{:S(2)}) copy-start(bf16[3,768,384]{1,2,0:T(8,128)(2,1)S(1)} %copy.142) | copy-start | bytes 5308420
  146.8 3.9 copy-start.69
  151.5 8.7 %copy-start.77 = (pred[384]{0:T(512)(128)(4,1)S(1)}, pred[384]{0:T(512)(128)(4,1)}, u32[]{:S(2)}) copy-start(pred[384]{0:T(512)(128)(4,1)} %broadcast_compare_fusion.1) | copy-start | bytes 1156
  176.8 7.0 %copy-start.5 = (f32[384,768]{1,0:T(8,128)}, f32[384,768]{1,0:T(8,128)S(1)}, u32[]{:S(2)}) copy-start(f32[384,768]{1,0:T(8,128)S(1)} %get-tuple-element.118) | copy-start | bytes 3538948
  176.8 7.0 %copy-start.55 = (f32[384]{0:T(512)}, f32[384]{0:T(512)S(1)}, u32[]{:S(2)}) copy-start(f32[384]{0:T(512)S(1)} %broadcast_multiply_fusion.2) | copy-start | bytes 4612
  177.1 6.7 %copy-start.59 = (f32[384]{0:T(512)}, f32[384]{0:T(512)S(1)}, u32[]{:S(2)}) copy-start(f32[384]{0:T(512)S(1)} %fusion.107) | copy-start | bytes 4612
  177.8 8.2 %copy-start.34 = (bf16[768,1536]{0,1:T(8,128)(2,1)S(1)}, bf16[768,1536]{0,1:T(8,128)(2,1)}, u32[]{:S(2)}) copy-start(bf16[768,1536]{0,1:T(8,128)(2,1)} %maximum_bitcast_fusion) | copy-start | bytes 7077892
  196.6 3.7 copy-start.89
  200.4 4.9 %copy-start.15 = (bf16[3,768,384]{1,2,0:T(8,128)(2,1)S(1)}, bf16[3,768,384]{1,2,0:T(8,128)(2,1)}, u32[]{:S(2)}) copy-start(bf16[3,768,384]{1,2,0:T(8,128)(2,1)} %copy-done.13) | copy-start | bytes 5308420
  200.4 4.9 %copy-start.18 = (bf16[3,768,384]{1,2,0:T(8,128)(2,1)S(1)}, bf16[3,768,384]{1,2,0:T(8,128)(2,1)}, u32[]{:S(2)}) copy-start(bf16[3,768,384]{1,2,0:T(8,128)(2,1)} %copy-done.16) | copy-start | bytes 5308420
  200.4 4.9 %copy-start.19 = (bf16[3,768,384]{1,2,0:T(8,128)(2,1)S(1)}, bf16[3,768,384]{1,2,0:T(8,128)(2,1)}, u32[]{:S(2)}) copy-start(bf16[3,768,384]{1,2,0:T(8,128)(2,1)} %copy.143) | copy-start | bytes 5308420
  200.4 4.9 %copy-start.20 = (bf16[3,768,384]{1,2,0:T(8,128)(2,1)S(1)}, bf16[3,768,384]{1,2,0:T(8,128)(2,1)}, u32[]{:S(2)}) copy-start(bf16[3,768,384]{1,2,0:T(8,128)(2,1)} %copy.144) | copy-start | bytes 5308420
  228.4 4.4 copy-start.91
  228.4 4.4 copy-start.93
  230.9 6.9 %slice-start.2 = ((s8[4718592]{0:T(1024)(128)(4,1)}), s8[4194304]{0:T(1024)(128)(4,1)S(1)}, s32[]{:S(2)}) async-start(s8[4718592]{0:T(1024)(128)(4,1)} %bitcast.157), calls=%async_computation.5 | async-start | bytes 8388608
  232.8 5.0 %copy-start.27 = (f32[384,768]{1,0:T(8,128)S(1)}, f32[384,768]{1,0:T(8,128)}, u32[]{:S(2)}) copy-start(f32[384,768]{1,0:T(8,128)} %copy-done.26) | copy-start | bytes 3538948
  232.8 5.0 %copy-start.81 = (f32[384]{0:T(512)S(1)}, f32[384]{0:T(512)}, u32[]{:S(2)}) copy-start(f32[384]{0:T(512)} %copy-done.80) | copy-start | bytes 4612
  232.8 5.0 %slice-start.3 = ((s8[4718592]{0:T(1024)(128)(4,1)}), s8[524288]{0:T(1024)(128)(4,1)S(1)}, s32[]{:S(2)}) async-start(s8[4718592]{0:T(1024)(128)(4,1)} %bitcast.157), calls=%async_computation.6 | async-start | bytes 1048576
  243.8 4.4 copy-start.9
  243.8 4.4 copy-start.64
  252.7 4.1 slice-start
  259.4 93.7 %copy-start.30 = (f32[384,768]{1,0:T(8,128)S(1)}, f32[384,768]{1,0:T(8,128)}, u32[]{:S(2)}) copy-start(f32[384,768]{1,0:T(8,128)} %get-tuple-element.109) | copy-start | bytes 3538948
  259.4 93.7 %copy-start.66 = (s32[384]{0:T(512)S(1)}, s32[384]{0:T(512)}, u32[]{:S(2)}) copy-start(s32[384]{0:T(512)} %copy-done.65) | copy-start | bytes 4612
  353.1 7.0 %copy-start.76 = (f32[768]{0:T(1024)S(1)}, f32[768]{0:T(1024)}, u32[]{:S(2)}) copy-start(f32[768]{0:T(1024)} %get-tuple-element.77) | copy-start | bytes 9220
  353.1 7.0 %copy-start.75 = (f32[768]{0:T(1024)S(1)}, f32[768]{0:T(1024)}, u32[]{:S(2)}) copy-start(f32[768]{0:T(1024)} %get-tuple-element.71) | copy-start | bytes 9220
  353.1 7.0 %copy-start.74 = (f32[768]{0:T(1024)S(1)}, f32[768]{0:T(1024)}, u32[]{:S(2)}) copy-start(f32[768]{0:T(1024)} %get-tuple-element.80) | copy-start | bytes 9220
  353.1 9.0 %copy-start.73 = (f32[768]{0:T(1024)S(1)}, f32[768]{0:T(1024)}, u32[]{:S(2)}) copy-start(f32[768]{0:T(1024)} %get-tuple-element.73) | copy-start | bytes 9220
  354.8 52.5 %copy-start.4 = (f32[4,48,384]{2,1,0:T(8,128)S(1)}, f32[4,48,384]{2,1,0:T(8,128)}, u32[]{:S(2)}) copy-start(f32[4,48,384]{2,1,0:T(8,128)} %refs_0_.1) | copy-start | bytes 884740
  354.8 52.5 %copy-start.50 = (f32[4,48,384]{2,1,0:T(8,128)S(1)}, f32[4,48,384]{2,1,0:T(8,128)}, u32[]{:S(2)}) copy-start(f32[4,48,384]{2,1,0:T(8,128)} %param.23) | copy-start | bytes 884740
  354.8 52.6 %copy-start.51 = (f32[4,48,384]{2,1,0:T(8,128)S(1)}, f32[4,48,384]{2,1,0:T(8,128)}, u32[]{:S(2)}) copy-start(f32[4,48,384]{2,1,0:T(8,128)} %param.24) | copy-start | bytes 884740
  354.8 56.4 %all-to-all-start.2 = ((f32[16,24,384]{2,1,0:T(8,128)}), f32[16,24,384]{2,1,0:T(8,128)}, u32[]{:S(2)}, u32[]{:S(2)}) async-start(f32[16,24,384]{2,1,0:T(8,128)} %bitcast.48), calls=%async_computation.2 | async-start | bytes 1179648 | tf_op jit(solution)/shard_map/all_to_all | solution.py:582
  408.8 60.9 %copy-start.45 = (f32[4,48,384]{2,1,0:T(8,128)}, f32[4,48,384]{2,1,0:T(8,128)S(1)}, u32[]{:S(2)}) copy-start(f32[4,48,384]{2,1,0:T(8,128)S(1)} %get-tuple-element.100) | copy-start | bytes 884740
  408.9 60.9 %copy-start.46 = (f32[4,48,384]{2,1,0:T(8,128)}, f32[4,48,384]{2,1,0:T(8,128)S(1)}, u32[]{:S(2)}) copy-start(f32[4,48,384]{2,1,0:T(8,128)S(1)} %get-tuple-element.101) | copy-start | bytes 884740
  411.3 57.1 %copy-start.28 = (f32[3,48,1536]{2,1,0:T(8,128)}, f32[3,48,1536]{2,1,0:T(8,128)S(1)}, u32[]{:S(2)}) copy-start(f32[3,48,1536]{2,1,0:T(8,128)S(1)} %get-tuple-element.103) | copy-start | bytes 2654212
  411.3 57.1 %copy-start.29 = (f32[3,48,1536]{2,1,0:T(8,128)}, f32[3,48,1536]{2,1,0:T(8,128)S(1)}, u32[]{:S(2)}) copy-start(f32[3,48,1536]{2,1,0:T(8,128)S(1)} %get-tuple-element.104) | copy-start | bytes 2654212
  411.3 8.7 %copy-start.85 = (f32[4]{0:T(128)S(1)}, f32[4]{0:T(128)}, u32[]{:S(2)}) copy-start(f32[4]{0:T(128)} %get-tuple-element.81) | copy-start | bytes 52
  411.3 8.6 %copy-start.87 = (f32[3]{0:T(128)S(1)}, f32[3]{0:T(128)}, u32[]{:S(2)}) copy-start(f32[3]{0:T(128)} %get-tuple-element.78) | copy-start | bytes 40
  411.3 9.4 %copy-start.84 = (f32[4]{0:T(128)S(1)}, f32[4]{0:T(128)}, u32[]{:S(2)}) copy-start(f32[4]{0:T(128)} %get-tuple-element.82) | copy-start | bytes 52
  411.3 9.3 %copy-start.86 = (f32[3]{0:T(128)S(1)}, f32[3]{0:T(128)}, u32[]{:S(2)}) copy-start(f32[3]{0:T(128)} %get-tuple-element.79) | copy-start | bytes 40
  411.3 49.4 %copy-start.54 = (f32[4,768]{1,0:T(4,128)S(1)}, f32[4,768]{1,0:T(4,128)}, u32[]{:S(2)}) copy-start(f32[4,768]{1,0:T(4,128)} %param.31) | copy-start | bytes 36868
  (53 other events, 117.6 us)
